TPU v7x, 768 devices: a whole 4x8x12 slice. The times are simulated.
768 devices in a mesh: dp: 8 (over x, core), ctx: 96 (over y, z).
Axes of the slice: x: 4, y: 8, z: 12, core: 2. Of those that a mesh axis runs over, the one named last changes fastest.
Arguments:
- queries: bfloat16 [8, 12288, 4096], P('dp', 'ctx'), may hold values from -250 to 250
- keys: bfloat16 [8, 12288, 512], P('dp', 'ctx'), may hold values from -4 to 4
- values: bfloat16 [8, 12288, 512], P('dp', 'ctx'), may hold values from -6 to 6
- logp_grad: bfloat16 [8, 12288, 4096], P('dp', 'ctx'), may hold values from -6 to 6
- response_ids: int32 [8, 12288], P('dp', 'ctx'), may hold values from 0 to 47, as said below
- sample_ids: int32 [8, 48], P('dp'), may hold values from 0 to 47, as said below
- rewards: float32 [8, 48], P('dp'), may hold values from 0 to 1
- new_logp: float32 [8, 12288], P('dp', 'ctx'), may hold values from -4 to 0
- old_logp: float32 [8, 12288], P('dp', 'ctx'), may hold values from -4 to 0
Outputs:
- query_grad: bfloat16 [8, 12288, 4096], P('dp', 'ctx')
- key_grad: bfloat16 [8, 12288, 512], P('dp', 'ctx')
- value_grad: bfloat16 [8, 12288, 512], P('dp', 'ctx')
- token_ratio: float32 [8, 12288], P('dp', 'ctx')
- advantage: float32 [8, 48], P('dp')
Inputs may be any that keep to these rules, and one draw needn't show every extreme that they name: `response_ids`: along each packed row the ids never fall; every id names 128 to 384 consecutive positions, and some id names exactly 384. `sample_ids`: each prompt id names exactly 8 responses of the whole batch.
All inputs are finite; a program needn't handle non-finite values.
Results may differ from a plain program's by a relative error of at most 0.015.
Values may be sent and summed in bfloat16 or wider, within the bound.
No kernel may reach another device: no remote copies, remote signals or barrier semaphores. Data moves between devices by JAX's collectives and lax.ppermute only.
A program may use at most 32 MiB of HBM per device.

v0:
```python
import math

import jax
import jax.numpy as jnp
from jax import lax
from jax.sharding import PartitionSpec as P

QHEADS = 32
KVHEADS = 4
HEAD_DIM = 128
SPAN = 3
GROUP = 8
MEAN_LEN = 256


def prefix(array, axis, combine, identity, reverse):
    count, index = (lax.axis_size(axis), lax.axis_index(axis))
    everything = jax.tree.map(lambda part: lax.all_gather(part, axis), array)
    start = jax.tree.map(
        lambda part, zero: jnp.broadcast_to(jnp.asarray(zero, part.dtype), part.shape),
        array,
        identity,
    )

    def lap(k, before):
        at = count - 1 - k if reverse else k
        reached = at > index if reverse else at < index
        new = combine(before, jax.tree.map(lambda part: part[at], everything))
        return jax.tree.map(lambda a, b: jnp.where(reached, a, b), new, before)

    return lax.fori_loop(0, count, lap, start)


def passed_along(array, axis, by):
    count = lax.axis_size(axis)
    pairs = [(i, i + by) for i in range(count) if 0 <= i + by < count]
    return lax.ppermute(array, axis, pairs)


def join_down(earlier, later):
    early_first, early_last, early_sum, early_count = earlier
    late_first, late_last, late_sum, late_count = later
    linked = (late_first == late_last) & (late_first == early_last)
    first_id = jnp.where(early_last < 0, late_first, early_first)
    tail_sum = jnp.where(linked, early_sum + late_sum, late_sum)
    tail_count = jnp.where(linked, early_count + late_count, late_count)
    late_empty = late_last < 0
    return (
        jnp.where(late_empty, early_first, first_id),
        jnp.where(late_empty, early_last, late_last),
        jnp.where(late_empty, early_sum, tail_sum),
        jnp.where(late_empty, early_count, tail_count),
    )


def join_up(earlier, later):
    high_first, high_last, high_sum, high_count = earlier
    low_first, low_last, low_sum, low_count = later
    linked = (low_first == low_last) & (low_last == high_first)
    head_sum = jnp.where(linked, low_sum + high_sum, low_sum)
    head_count = jnp.where(linked, low_count + high_count, low_count)
    last_id = jnp.where(high_last < 0, low_last, high_last)
    low_empty = low_last < 0
    return (
        jnp.where(low_empty, high_first, low_first),
        jnp.where(low_empty, high_last, last_id),
        jnp.where(low_empty, high_sum, head_sum),
        jnp.where(low_empty, high_count, head_count),
    )


def shards(queries, keys, values, logp_grad, response_ids, sample_ids, rewards, new_logp, old_logp):
    highest = lax.Precision.HIGHEST
    tok_rows = queries.shape[1]
    shard_index = lax.axis_index("ctx")
    offset = shard_index * tok_rows
    token_ids = response_ids[0]
    log_ratio = new_logp[0] - old_logp[0]
    resp_count = rewards.shape[1]
    group_count = lax.axis_size("dp") * resp_count // GROUP
    resp_range = jnp.arange(resp_count, dtype=jnp.int32)
    sample_hot = (
        sample_ids[0][:, None] == jnp.arange(group_count, dtype=jnp.int32)[None, :]
    ).astype(jnp.float32)
    own_rewards = rewards[0]
    first_id = token_ids[0]
    last_id = token_ids[-1]
    in_first = (token_ids == first_id).astype(jnp.float32)
    in_last = (token_ids == last_id).astype(jnp.float32)
    head_sum = jnp.sum(log_ratio * in_first)
    head_count = jnp.sum(in_first)
    tail_sum = jnp.sum(log_ratio * in_last)
    tail_count = jnp.sum(in_last)
    first_val = first_id.astype(jnp.float32)
    last_val = last_id.astype(jnp.float32)
    neg_one = jnp.float32(-1.0)
    zero_val = jnp.float32(0.0)
    below = prefix(
        (first_val, last_val, tail_sum, tail_count),
        "ctx",
        join_down,
        (neg_one, neg_one, zero_val, zero_val),
        False,
    )
    above = prefix(
        (first_val, last_val, head_sum, head_count),
        "ctx",
        join_up,
        (neg_one, neg_one, zero_val, zero_val),
        True,
    )
    from_below = jnp.where(below[1] == first_val, below[2], 0.0)
    count_below = jnp.where(below[1] == first_val, below[3], 0.0)
    from_above = jnp.where(above[0] == last_val, above[2], 0.0)
    count_above = jnp.where(above[0] == last_val, above[3], 0.0)
    single = first_id == last_id
    first_total = head_sum + from_below + jnp.where(single, from_above, 0.0)
    first_count = head_count + count_below + jnp.where(single, count_above, 0.0)
    last_total = tail_sum + from_above + jnp.where(single, from_below, 0.0)
    last_count = tail_count + count_above + jnp.where(single, count_below, 0.0)
    group_sums = lax.psum(jnp.dot(own_rewards, sample_hot, precision=highest), "dp")
    advantage = own_rewards - jnp.dot(sample_hot, group_sums, precision=highest) / GROUP
    first_adv = jnp.sum(jnp.where(resp_range == first_id, advantage, 0.0))
    last_adv = jnp.sum(jnp.where(resp_range == last_id, advantage, 0.0))
    is_first = token_ids == first_id
    tok_total = jnp.where(is_first, first_total, last_total)
    tok_count = jnp.where(is_first, first_count, last_count)
    tok_ratio = jnp.exp(tok_total / tok_count)
    tok_adv = jnp.where(is_first, first_adv, last_adv)
    tok_start = jnp.where(
        is_first,
        offset - count_below.astype(jnp.int32),
        offset + tok_rows - tail_count.astype(jnp.int32),
    )
    tok_weight = -tok_adv * tok_ratio * MEAN_LEN / tok_count
    out_grad = (tok_weight[:, None] * logp_grad[0].astype(jnp.float32)).astype(jnp.bfloat16)
    own_keys = keys[0]
    own_values = values[0]
    arrived = [
        passed_along((own_keys, own_values), "ctx", distance) for distance in range(1, SPAN + 1)
    ]
    ordered = arrived[::-1]
    key_window = jnp.concatenate([piece[0] for piece in ordered] + [own_keys], axis=0)
    value_window = jnp.concatenate([piece[1] for piece in ordered] + [own_values], axis=0)
    window_rows = key_window.shape[0]
    key_pos = offset - SPAN * tok_rows + jnp.arange(window_rows, dtype=jnp.int32)
    query_pos = offset + jnp.arange(tok_rows, dtype=jnp.int32)
    allowed = (key_pos[None, :] <= query_pos[:, None]) & (key_pos[None, :] >= tok_start[:, None])
    score_scale = 1.0 / math.sqrt(HEAD_DIM)
    group_heads = QHEADS // KVHEADS
    query_heads = queries[0].reshape(tok_rows, KVHEADS, group_heads, HEAD_DIM)
    grad_heads = out_grad.reshape(tok_rows, KVHEADS, group_heads, HEAD_DIM)
    query_parts = []
    key_parts = []
    value_parts = []
    for kv_head in range(KVHEADS):
        query_group = query_heads[:, kv_head]
        grad_group = grad_heads[:, kv_head]
        key_group = key_window[:, kv_head * HEAD_DIM : (kv_head + 1) * HEAD_DIM]
        value_group = value_window[:, kv_head * HEAD_DIM : (kv_head + 1) * HEAD_DIM]
        scores = (
            jnp.einsum("thd,jd->htj", query_group, key_group, preferred_element_type=jnp.float32)
            * score_scale
        )
        scores = jnp.where(allowed[None], scores, -jnp.inf)
        row_top = jnp.max(scores, axis=-1, keepdims=True)
        powers = jnp.exp(scores - row_top)
        row_sum = jnp.sum(powers, axis=-1, keepdims=True)
        weights = powers / row_sum
        weights_bf = weights.astype(jnp.bfloat16)
        attended = jnp.einsum(
            "htj,jd->thd", weights_bf, value_group, preferred_element_type=jnp.float32
        )
        row_delta = jnp.sum(grad_group.astype(jnp.float32) * attended, axis=-1).T
        dprob = jnp.einsum(
            "thd,jd->htj", grad_group, value_group, preferred_element_type=jnp.float32
        )
        dscore = (weights * (dprob - row_delta[:, :, None])).astype(jnp.bfloat16)
        query_parts.append(
            jnp.einsum("htj,jd->thd", dscore, key_group, preferred_element_type=jnp.float32)
            * score_scale
        )
        key_parts.append(
            jnp.einsum("htj,thd->jd", dscore, query_group, preferred_element_type=jnp.float32)
            * score_scale
        )
        value_parts.append(
            jnp.einsum("htj,thd->jd", weights_bf, grad_group, preferred_element_type=jnp.float32)
        )
    query_grad = (
        jnp.stack(query_parts, axis=1).reshape(tok_rows, QHEADS * HEAD_DIM).astype(jnp.bfloat16)
    )
    key_full = jnp.concatenate(key_parts, axis=1)
    value_full = jnp.concatenate(value_parts, axis=1)

    def rows_for(matrix, distance):
        return matrix[(SPAN - distance) * tok_rows : (SPAN - distance + 1) * tok_rows]

    key_sum = rows_for(key_full, 0)
    value_sum = rows_for(value_full, 0)
    for distance in range(1, SPAN + 1):
        back_keys, back_values = (
            passed_along(
                rows_for(key_full, distance).astype(jnp.bfloat16), "ctx", -distance
            ).astype(jnp.float32),
            passed_along(
                rows_for(value_full, distance).astype(jnp.bfloat16), "ctx", -distance
            ).astype(jnp.float32),
        )
        key_sum = key_sum + back_keys
        value_sum = value_sum + back_values
    return (
        query_grad[None],
        key_sum.astype(jnp.bfloat16)[None],
        value_sum.astype(jnp.bfloat16)[None],
        tok_ratio[None],
        advantage[None],
    )


def solution(mesh):
    return jax.shard_map(
        shards,
        mesh=mesh,
        in_specs=(
            P("dp", "ctx", None),
            P("dp", "ctx", None),
            P("dp", "ctx", None),
            P("dp", "ctx", None),
            P("dp", "ctx"),
            P("dp", None),
            P("dp", None),
            P("dp", "ctx"),
            P("dp", "ctx"),
        ),
        out_specs=(
            P("dp", "ctx", None),
            P("dp", "ctx", None),
            P("dp", "ctx", None),
            P("dp", "ctx"),
            P("dp", None),
        ),
        check_vma=False,
    )
```

profile of v0, /device:TPU:96, one launch (start us, length us, event | category | flops | bytes accessed | tf_op | source)
XLA Modules:
  0.0 1908.6 jit_solution(5434096379746569414)
XLA Ops:
  0.6 4.4 collective-permute-start.2
  5.1 7.3 collective-permute-start.1
  12.4 7.6 collective-permute-start
  20.0 3.4 collective-permute-start.5
  23.4 4.3 collective-permute-start.4
  27.7 1.3 fusion.88
  31.6 2.6 select_reduce_fusion
  34.8 1.3 dynamic-slice
  37.4 1.3 dynamic-update-slice.4
  38.7 1.3 dynamic-update-slice.2
  40.0 1.2 dynamic-update-slice.3
  41.3 1.3 dynamic-update-slice.5
  42.6 206.8 %all-reduce.6 = (f32[96]{0:T(128)S(1)}, f32[96]{0:T(128)S(1)}, f32[96]{0:T(128)S(1)}, f32[96]{0:T(128)S(1)}, f32[96]{0:T(128)S(1)}, /*index=5*/f32[96]{0:T(128)S(1)}) all-reduce(f32[96]{0:T(128)S(1)} %dynamic-update-slice, f32[96]{0:T(128)S(1)} %dynamic-update-slice.1, ...), channel_id=1, replica_groups=mesh['dp'=8,'ctx'=96] {'ctx'}, use_global_device_ids=true, to_apply=%add | all-reduce | flops 576 | bytes 4608
  249.4 747.0 %while.36 = (s32[]{:T(128)}, f32[]{:T(128)}, f32[]{:T(128)}, f32[]{:T(128)}, s32[]{:T(128)}, /*index=5*/f32[96]{0:T(128)S(1)}, f32[96]{0:T(128)S(1)}, f32[96]{0:...) while((s32[]{:T(128)}, f32[]{:T(128)}, f32[]{:T(128)}, f32[]{:T(128)}, s32[]{:T(128)}, ...), condition=%wide.region_3.0_spmd, body=%wide.region_2.0_spmd.sunk | while | flops 17 | bytes 340 | solution.py:31
  997.9 12.4 psum.7
  1010.3 3.4 fusion.74
  1014.4 792.3 %while.37 = (s32[]{:T(128)}, f32[]{:T(128)}, f32[]{:T(128)}, f32[]{:T(128)}, s32[]{:T(128)}, /*index=5*/f32[96]{0:T(128)S(1)}, f32[96]{0:T(128)S(1)}, f32[96]{0:...) while((s32[]{:T(128)}, f32[]{:T(128)}, f32[]{:T(128)}, ...), condition=%wide.region_12.13_spmd, body=%wide.region_11.12_spmd.sunk | while | flops 21 | bytes 402 | solution.py:31
  1807.9 2.3 copy.53
  1811.5 1.3 bitcast_divide_fusion
  1812.8 1.3 multiply_convert_fusion
  1814.8 2.1 collective-permute-start.3
  1816.9 1.1 pad_maximum_fusion.3
  1818.8 2.1 fusion.91
  1820.9 1.9 fusion.51
  1823.3 5.2 collective-permute-done.3
  1831.1 2.0 fusion.34
  1833.1 3.0 fusion.90
  1836.1 1.8 fusion.52
  1840.0 1.2 fusion.29
  1841.2 1.9 fusion.33
  1843.1 3.0 fusion.89
  1846.1 1.8 fusion.53
  1850.0 1.2 fusion.28
  1851.2 1.9 fusion.32
  1853.1 3.0 fusion.92
  1856.1 1.8 fusion.50
  1860.5 1.2 fusion.35
  1863.9 1.3 copy.96
  1865.3 8.2 collective-permute-start.6
  1873.5 1.9 collective-permute-start.8
  1875.4 1.9 collective-permute-start.7
  1877.5 2.1 collective-permute-start.9
  1879.6 1.9 collective-permute-start.11
  1881.6 5.7 collective-permute-start.10
  1887.3 4.4 collective-permute-done.7
  1893.5 4.1 collective-permute-done.9
  1897.6 7.0 collective-permute-done.11
  1904.6 3.1 collective-permute-done.10
  (857 shorter events, 477.1 us)
Async XLA Ops:
  0.6 1809.6 %copy-start.10 = (bf16[1,128,4096]{2,1,0:T(8,128)(2,1)S(1)}, bf16[1,128,4096]{2,1,0:T(8,128)(2,1)}, u32[]{:S(2)}) copy-start(bf16[1,128,4096]{2,1,0:T(8,128)(2,1)} %param.16) | copy-start | bytes 3145732
  0.6 1814.2 %collective-permute-start.2 = (bf16[128,512]{1,0:T(8,128)(2,1)}, bf16[128,512]{1,0:T(8,128)(2,1)}, u32[]{:S(2)}, u32[]{:S(2)}) collective-permute-start(bf16[128,512]{1,0:T(8,128)(2,1)} %bitcast.370), channel_id=1, source_target_pairs={{0,1},{1,2},{2,3},{3,4},{4,5},{5,6},{6,7},{7,8},{8,9},{9,10},{10,1... | collective-permute-start | bytes 393224 | tf_op jit(solution)/shard_map/ppermute | solution.py:37
  5.1 1811.8 %collective-permute-start.1 = (bf16[128,512]{1,0:T(8,128)(2,1)}, bf16[128,512]{1,0:T(8,128)(2,1)}, u32[]{:S(2)}, u32[]{:S(2)}) collective-permute-start(bf16[128,512]{1,0:T(8,128)(2,1)} %bitcast.371), channel_id=1, source_target_pairs={{0,2},{1,3},{2,4},{3,5},{4,6},{5,7},{6,8},{7,9},{8,10},{9,11},{10,... | collective-permute-start | bytes 393224 | tf_op jit(solution)/shard_map/ppermute | solution.py:37
  12.4 1804.5 %collective-permute-start = (bf16[128,512]{1,0:T(8,128)(2,1)}, bf16[128,512]{1,0:T(8,128)(2,1)}, u32[]{:S(2)}, u32[]{:S(2)}) collective-permute-start(bf16[128,512]{1,0:T(8,128)(2,1)} %bitcast.372), channel_id=1, source_target_pairs={{0,3},{1,4},{2,5},{3,6},{4,7},{5,8},{6,9},{7,10},{8,11},{9,12},{10... | collective-permute-start | bytes 393224 | tf_op jit(solution)/shard_map/ppermute | solution.py:37
  20.0 1803.3 %collective-permute-start.5 = (bf16[128,512]{1,0:T(8,128)(2,1)}, bf16[128,512]{1,0:T(8,128)(2,1)}, u32[]{:S(2)}, u32[]{:S(2)}) collective-permute-start(bf16[128,512]{1,0:T(8,128)(2,1)} %bitcast.374), channel_id=1, source_target_pairs={{0,1},{1,2},{2,3},{3,4},{4,5},{5,6},{6,7},{7,8},{8,9},{9,10},{10,1... | collective-permute-start | bytes 393224 | tf_op jit(solution)/shard_map/ppermute | solution.py:37
  23.4 1799.9 %collective-permute-start.4 = (bf16[128,512]{1,0:T(8,128)(2,1)}, bf16[128,512]{1,0:T(8,128)(2,1)}, u32[]{:S(2)}, u32[]{:S(2)}) collective-permute-start(bf16[128,512]{1,0:T(8,128)(2,1)} %bitcast.375), channel_id=1, source_target_pairs={{0,2},{1,3},{2,4},{3,5},{4,6},{5,7},{6,8},{7,9},{8,10},{9,11},{10,... | collective-permute-start | bytes 393224 | tf_op jit(solution)/shard_map/ppermute | solution.py:37
  1811.4 3.4 copy-start.19
  1811.4 5.5 copy-start.18
  1812.8 6.0 copy-start
  1814.8 13.7 collective-permute-start.3
  1818.0 0.8 copy-start.8
  1820.9 1.9 copy-start.1
  1822.8 7.4 copy-start.4
  1829.5 1.1 copy-start.14
  1836.1 1.8 copy-start.15
  1837.9 1.6 copy-start.6
  1846.1 1.8 copy-start.16
  1847.9 1.6 copy-start.7
  1856.1 1.8 copy-start.17
  1857.9 1.6 copy-start.5
  1860.0 1.8 copy-start.2
  1860.0 1.8 copy-start.3
  1861.8 2.0 copy-start.11
  1861.8 2.0 copy-start.12
  1861.8 2.0 copy-start.13
  1863.8 1.5 copy-start.9
  1865.3 16.3 collective-permute-start.6
  1873.5 13.8 collective-permute-start.8
  1875.4 16.3 collective-permute-start.7
  1877.5 20.1 %collective-permute-start.9 = (bf16[128,512]{0,1:T(8,128)(2,1)S(1)}, bf16[128,512]{0,1:T(8,128)(2,1)S(1)}, u32[]{:S(2)}, u32[]{:S(2)}) collective-permute-start(bf16[128,512]{0,1:T(8,128)(2,1)S(1)} %get-tuple-element.448), channel_id=1, source_target_pairs={{1,0},{2,1},{3,2},{4,3},{5,4},{6,5},{7,6},{8,7},{9,8},{10,9},{11,1... | collective-permute-start | bytes 393224 | tf_op jit(solution)/shard_map/ppermute | solution.py:37
  1879.6 25.0 %collective-permute-start.11 = (bf16[128,512]{0,1:T(8,128)(2,1)S(1)}, bf16[128,512]{0,1:T(8,128)(2,1)S(1)}, u32[]{:S(2)}, u32[]{:S(2)}) collective-permute-start(bf16[128,512]{0,1:T(8,128)(2,1)S(1)} %get-tuple-element.449), channel_id=1, source_target_pairs={{3,0},{4,1},{5,2},{6,3},{7,4},{8,5},{9,6},{10,7},{11,8},{12,9},{13... | collective-permute-start | bytes 393224 | tf_op jit(solution)/shard_map/ppermute | solution.py:37
  1881.6 26.1 %collective-permute-start.10 = (bf16[128,512]{0,1:T(8,128)(2,1)S(1)}, bf16[128,512]{0,1:T(8,128)(2,1)S(1)}, u32[]{:S(2)}, u32[]{:S(2)}) collective-permute-start(bf16[128,512]{0,1:T(8,128)(2,1)S(1)} %get-tuple-element.450), channel_id=1, source_target_pairs={{2,0},{3,1},{4,2},{5,3},{6,4},{7,5},{8,6},{9,7},{10,8},{11,9},{12,... | collective-permute-start | bytes 393224 | tf_op jit(solution)/shard_map/ppermute | solution.py:37
where the time goes:
time: 1920 us; the launch traced here: 1910 us
  loops' own time  1080 us (56%)
  local copies, waits for them, and re-layouts  475 us (25%)
  blocking collectives  219 us (11%)
  starting transfers between devices  50.9 us (3%)
  matrix products  32 us (2%)
  waiting for transfers between devices  23.8 us (1%)
    another operation x2, loops' own time, prefix(): return lax.fori_loop(0, count, lap, start)  1080 us
    dynamic_slice x768, local copies, waits for them, and re-layouts, lap(): new = combine(before, jax.tree.map(lambda part: part[at], everything))  458 us
    unnamed x1, blocking collectives  207 us
    ppermute x12, starting transfers between devices, passed_along(): return lax.ppermute(array, axis, pairs)  50.9 us
  transfers between devices with their start and end apart: 12, of which 5 were waited for; matrix products, arithmetic and copies ran while one was open for 26% of the time, Pallas kernels for 0%

commit v1 on v0

v1 whole, which is shorter than its diff:
```python
import math

import jax
import jax.numpy as jnp
from jax import lax
from jax.sharding import PartitionSpec as P

QHEADS = 32
KVHEADS = 4
HEAD_DIM = 128
SPAN = 3
GROUP = 8
MEAN_LEN = 256


def passed_along(array, axis, by):
    count = lax.axis_size(axis)
    pairs = [(i, i + by) for i in range(count) if 0 <= i + by < count]
    return lax.ppermute(array, axis, pairs)


def summed_over_dp(array):
    count = lax.axis_size("dp")
    step = 1
    while step < count:
        array = array + lax.ppermute(array, "dp", [(i, i ^ step) for i in range(count)])
        step *= 2
    return array


def shards(queries, keys, values, logp_grad, response_ids, sample_ids, rewards, new_logp, old_logp):
    highest = lax.Precision.HIGHEST
    tok_rows = queries.shape[1]
    ids = response_ids[0] + 1
    log_ratio = new_logp[0] - old_logp[0]
    own_keys = keys[0]
    own_values = values[0]
    arrived = [
        passed_along((own_keys, own_values), "ctx", distance) for distance in range(1, SPAN + 1)
    ]
    info = jnp.stack([ids.astype(jnp.float32), log_ratio])
    below = [passed_along(info, "ctx", distance) for distance in range(SPAN, 0, -1)]
    above = [passed_along(info, "ctx", -distance) for distance in range(1, SPAN + 1)]
    window = jnp.stack(below + [info] + above)
    window_ids = window[:, 0]
    window_logs = window[:, 1]
    first_id = info[0, 0]
    last_id = info[0, tok_rows - 1]
    of_first = window_ids == first_id
    of_last = window_ids == last_id
    first_count = jnp.sum(of_first.astype(jnp.float32))
    last_count = jnp.sum(of_last.astype(jnp.float32))
    first_total = jnp.sum(jnp.where(of_first, window_logs, 0.0))
    last_total = jnp.sum(jnp.where(of_last, window_logs, 0.0))
    resp_count = rewards.shape[1]
    group_count = lax.axis_size("dp") * resp_count // GROUP
    sample_hot = (
        sample_ids[0][:, None] == jnp.arange(group_count, dtype=jnp.int32)[None, :]
    ).astype(jnp.float32)
    own_rewards = rewards[0]
    group_sums = summed_over_dp(jnp.dot(own_rewards, sample_hot, precision=highest))
    advantage = own_rewards - jnp.dot(sample_hot, group_sums, precision=highest) / GROUP
    resp_range = jnp.arange(resp_count, dtype=jnp.int32) + 1
    first_adv = jnp.sum(jnp.where(resp_range == ids[0], advantage, 0.0))
    last_adv = jnp.sum(jnp.where(resp_range == ids[-1], advantage, 0.0))
    is_first = ids == ids[0]
    tok_total = jnp.where(is_first, first_total, last_total)
    tok_count = jnp.where(is_first, first_count, last_count)
    tok_ratio = jnp.exp(tok_total / tok_count)
    tok_adv = jnp.where(is_first, first_adv, last_adv)
    tok_weight = -tok_adv * tok_ratio * MEAN_LEN / tok_count
    ordered = arrived[::-1]
    key_window = jnp.concatenate([piece[0] for piece in ordered] + [own_keys], axis=0)
    value_window = jnp.concatenate([piece[1] for piece in ordered] + [own_values], axis=0)
    window_rows = key_window.shape[0]
    key_pos = jnp.arange(window_rows, dtype=jnp.int32) - SPAN * tok_rows
    query_pos = jnp.arange(tok_rows, dtype=jnp.int32)
    key_ids = window_ids[: SPAN + 1].reshape(window_rows)
    allowed = (key_pos[None, :] <= query_pos[:, None]) & (key_ids[None, :] == info[0][:, None])
    score_scale = 1.0 / math.sqrt(HEAD_DIM)
    group_heads = QHEADS // KVHEADS
    query_heads = queries[0].reshape(tok_rows, KVHEADS, group_heads, HEAD_DIM)
    grad_heads = logp_grad[0].reshape(tok_rows, KVHEADS, group_heads, HEAD_DIM)
    query_parts = []
    key_parts = []
    value_parts = []
    for kv_head in range(KVHEADS):
        query_group = query_heads[:, kv_head]
        grad_group = grad_heads[:, kv_head]
        key_group = key_window[:, kv_head * HEAD_DIM : (kv_head + 1) * HEAD_DIM]
        value_group = value_window[:, kv_head * HEAD_DIM : (kv_head + 1) * HEAD_DIM]
        scores = (
            jnp.einsum("thd,jd->htj", query_group, key_group, preferred_element_type=jnp.float32)
            * score_scale
        )
        scores = jnp.where(allowed[None], scores, -jnp.inf)
        row_top = jnp.max(scores, axis=-1, keepdims=True)
        powers = jnp.exp(scores - row_top)
        row_sum = jnp.sum(powers, axis=-1, keepdims=True)
        weights = powers / row_sum
        weights_bf = weights.astype(jnp.bfloat16)
        dprob = jnp.einsum(
            "thd,jd->htj", grad_group, value_group, preferred_element_type=jnp.float32
        )
        row_delta = jnp.sum(weights_bf.astype(jnp.float32) * dprob, axis=-1, keepdims=True)
        dscore = (weights * (dprob - row_delta)).astype(jnp.bfloat16)
        query_parts.append(
            jnp.einsum("htj,jd->thd", dscore, key_group, preferred_element_type=jnp.float32)
        )
        key_parts.append(
            jnp.einsum("htj,thd->jd", dscore, query_group, preferred_element_type=jnp.float32)
        )
        value_parts.append(
            jnp.einsum("htj,thd->jd", weights_bf, grad_group, preferred_element_type=jnp.float32)
        )
    scaled_weight = (tok_weight * score_scale)[:, None]
    query_grad = (
        jnp.stack(query_parts, axis=1).reshape(tok_rows, QHEADS * HEAD_DIM) * scaled_weight
    ).astype(jnp.bfloat16)
    key_full = jnp.concatenate(key_parts, axis=1)
    value_full = jnp.concatenate(value_parts, axis=1)

    def rows_for(matrix, distance):
        return matrix[(SPAN - distance) * tok_rows : (SPAN - distance + 1) * tok_rows]

    key_sum = rows_for(key_full, 0)
    value_sum = rows_for(value_full, 0)
    for distance in range(1, SPAN + 1):
        key_sum = key_sum + passed_along(
            rows_for(key_full, distance).astype(jnp.bfloat16), "ctx", -distance
        ).astype(jnp.float32)
        value_sum = value_sum + passed_along(
            rows_for(value_full, distance).astype(jnp.bfloat16), "ctx", -distance
        ).astype(jnp.float32)
    return (
        query_grad[None],
        (key_sum * scaled_weight).astype(jnp.bfloat16)[None],
        (value_sum * tok_weight[:, None]).astype(jnp.bfloat16)[None],
        tok_ratio[None],
        advantage[None],
    )


def solution(mesh):
    return jax.shard_map(
        shards,
        mesh=mesh,
        in_specs=(
            P("dp", "ctx", None),
            P("dp", "ctx", None),
            P("dp", "ctx", None),
            P("dp", "ctx", None),
            P("dp", "ctx"),
            P("dp", None),
            P("dp", None),
            P("dp", "ctx"),
            P("dp", "ctx"),
        ),
        out_specs=(
            P("dp", "ctx", None),
            P("dp", "ctx", None),
            P("dp", "ctx", None),
            P("dp", "ctx"),
            P("dp", None),
        ),
        check_vma=False,
    )
```

time: 1920 us -> 176 us (0.09)
  the two profiles are of different devices: /device:TPU:96 before, /device:TPU:32 now
where the time goes in v1:
time: 176 us; the launch traced here: 175 us
  starting transfers between devices  87.8 us (50%)
  matrix products  35.1 us (20%)
  other arithmetic  23.6 us (13%)
  waiting for transfers between devices  17.5 us (10%)
  local copies, waits for them, and re-layouts  9.29 us (5%)
    ppermute x18, starting transfers between devices, passed_along(): return lax.ppermute(array, axis, pairs)  77.4 us
    ppermute x18, waiting for transfers between devices, passed_along(): return lax.ppermute(array, axis, pairs)  15.5 us
    ppermute x3, starting transfers between devices, summed_over_dp(): lax.ppermute(array, 'dp', [(i, i ^ step) for i in range(count)])  10.4 us
    dot_general x4, matrix products, shards(): jnp.einsum('htj,thd->jd', weights_bf, grad_group, preferred_element_type=...  10.3 us
    sub x4, matrix products, shards(): powers = jnp.exp(scores - row_top)  7.93 us
    dot_general x4, matrix products, shards(): jnp.einsum('thd,jd->htj', grad_group, value_group, preferred_element_type...  7.58 us
    unnamed x43, local copies, waits for them, and re-layouts  4.66 us
    mul x1, other arithmetic, shards(): scaled_weight = (tok_weight * score_scale)[:, None]  4.39 us
  transfers between devices with their start and end apart: 21, of which 6 were waited for; matrix products, arithmetic and copies ran while one was open for 18% of the time, Pallas kernels for 0%

profile of v1, /device:TPU:32, one launch (start us, length us, event | category | flops | bytes accessed | tf_op | source)
XLA Modules:
  0.0 174.6 jit_solution(8943908603843630214)
XLA Ops:
  2.1 14.5 %collective-permute-start.13 = (f32[2,128]{1,0:T(2,128)S(1)}, f32[2,128]{1,0:T(2,128)S(1)}, u32[]{:S(2)}, u32[]{:S(2)}) collective-permute-start(f32[2,128]{1,0:T(2,128)S(1)} %get-tuple-element.29), channel_id=1, source_target_pairs={{2,0},{3,1},{4,2},{5,3},{6,4},{7,5},{8,6},{9,7},{10,8},{11,9},{12,... | collective-permute-start | bytes 3080 | tf_op jit(solution)/shard_map/ppermute | solution.py:19
  16.5 2.5 %collective-permute-start.12 = (f32[2,128]{1,0:T(2,128)S(1)}, f32[2,128]{1,0:T(2,128)S(1)}, u32[]{:S(2)}, u32[]{:S(2)}) collective-permute-start(f32[2,128]{1,0:T(2,128)S(1)} %get-tuple-element.29), channel_id=1, source_target_pairs={{1,0},{2,1},{3,2},{4,3},{5,4},{6,5},{7,6},{8,7},{9,8},{10,9},{11,1... | collective-permute-start | bytes 3080 | tf_op jit(solution)/shard_map/ppermute | solution.py:19
  19.0 3.1 %collective-permute-start.14 = (f32[2,128]{1,0:T(2,128)S(1)}, f32[2,128]{1,0:T(2,128)S(1)}, u32[]{:S(2)}, u32[]{:S(2)}) collective-permute-start(f32[2,128]{1,0:T(2,128)S(1)} %get-tuple-element.29), channel_id=1, source_target_pairs={{3,0},{4,1},{5,2},{6,3},{7,4},{8,5},{9,6},{10,7},{11,8},{12,9},{13... | collective-permute-start | bytes 3080 | tf_op jit(solution)/shard_map/ppermute | solution.py:19
  22.1 3.9 %collective-permute-start.5 = (f32[2,128]{1,0:T(2,128)S(1)}, f32[2,128]{1,0:T(2,128)S(1)}, u32[]{:S(2)}, u32[]{:S(2)}) collective-permute-start(f32[2,128]{1,0:T(2,128)S(1)} %get-tuple-element.29), channel_id=1, source_target_pairs={{0,1},{1,2},{2,3},{3,4},{4,5},{5,6},{6,7},{7,8},{8,9},{9,10},{10,1... | collective-permute-start | bytes 3080 | tf_op jit(solution)/shard_map/ppermute | solution.py:19
  26.9 1.9 %collective-permute-start.9 = (f32[48]{0:T(128)S(1)}, f32[48]{0:T(128)S(1)}, u32[]{:S(2)}, u32[]{:S(2)}) collective-permute-start(f32[48]{0:T(128)S(1)} %convolution_bitcast_fusion.13), channel_id=1, source_target_pairs={{0,96},{96,0},{192,288},{288,192},{384,480},{480,384},{576,672},{6... | collective-permute-start | bytes 584 | tf_op jit(solution)/shard_map/ppermute | solution.py:26
  30.0 3.4 %collective-permute-start.10 = (f32[48]{0:T(128)S(1)}, f32[48]{0:T(128)S(1)}, u32[]{:S(2)}, u32[]{:S(2)}) collective-permute-start(f32[48]{0:T(128)S(1)} %add.63), channel_id=1, source_target_pairs={{0,192},{96,288},{192,0},{288,96},{384,576},{480,672},{576,384},{6... | collective-permute-start | bytes 584 | tf_op jit(solution)/shard_map/ppermute | solution.py:26
  33.4 2.0 %collective-permute-done.10 = f32[48]{0:T(128)S(1)} collective-permute-done((f32[48]{0:T(128)S(1)}, f32[48]{0:T(128)S(1)}, u32[]{:S(2)}, u32[]{:S(2)}) %collective-permute-start.10) | collective-permute-done | bytes 224 | tf_op jit(solution)/shard_map/ppermute | solution.py:26
  35.5 5.1 %collective-permute-start.11 = (f32[48]{0:T(128)S(1)}, f32[48]{0:T(128)S(1)}, u32[]{:S(2)}, u32[]{:S(2)}) collective-permute-start(f32[48]{0:T(128)S(1)} %add.64), channel_id=1, source_target_pairs={{0,384},{96,480},{192,576},{288,672},{384,0},{480,96},{576,192},{6... | collective-permute-start | bytes 584 | tf_op jit(solution)/shard_map/ppermute | solution.py:26
  40.6 1.6 copy.41
  42.2 1.3 copy.43
  43.5 5.2 %collective-permute-start.3 = (f32[2,128]{1,0:T(2,128)S(1)}, f32[2,128]{1,0:T(2,128)S(1)}, u32[]{:S(2)}, u32[]{:S(2)}) collective-permute-start(f32[2,128]{1,0:T(2,128)S(1)} %get-tuple-element.29), channel_id=1, source_target_pairs={{0,3},{1,4},{2,5},{3,6},{4,7},{5,8},{6,9},{7,10},{8,11},{9,12},{10... | collective-permute-start | bytes 3080 | tf_op jit(solution)/shard_map/ppermute | solution.py:19
  48.8 2.7 %fusion.67 = (f32[]{:T(128)}, f32[]{:T(128)}, f32[48]{0:T(128)}) fusion(s32[]{:T(128)} %bitcast.47, s32[]{:T(128)} %bitcast.54, f32[48]{0:T(128)S(1)} %add.64, f32[48]{0:T(128)S(1)} %collective-permute-done.11, s32[48]{0:T(128)S(1)} %bitcast.407, f32[1,48]{1,0:T(1,128)S(1)} %copy-done.16), kind=kOutput, calls=%fused_computation.145 | convolution fusion | flops 30430 | bytes 976 | tf_op jit(solution)/shard_map/dot_general | solution.py:62
  51.5 2.7 %collective-permute-done.3 = f32[2,128]{1,0:T(2,128)S(1)} collective-permute-done((f32[2,128]{1,0:T(2,128)S(1)}, f32[2,128]{1,0:T(2,128)S(1)}, u32[]{:S(2)}, u32[]{:S(2)}) %collective-permute-start.3) | collective-permute-done | bytes 1056 | tf_op jit(solution)/shard_map/ppermute | solution.py:19
  54.1 3.1 %collective-permute-start.4 = (f32[2,128]{1,0:T(2,128)S(1)}, f32[2,128]{1,0:T(2,128)S(1)}, u32[]{:S(2)}, u32[]{:S(2)}) collective-permute-start(f32[2,128]{1,0:T(2,128)S(1)} %get-tuple-element.29), channel_id=1, source_target_pairs={{0,2},{1,3},{2,4},{3,5},{4,6},{5,7},{6,8},{7,9},{8,10},{9,11},{10,... | collective-permute-start | bytes 3080 | tf_op jit(solution)/shard_map/ppermute | solution.py:19
  57.2 6.6 %collective-permute-done.4 = f32[2,128]{1,0:T(2,128)S(1)} collective-permute-done((f32[2,128]{1,0:T(2,128)S(1)}, f32[2,128]{1,0:T(2,128)S(1)}, u32[]{:S(2)}, u32[]{:S(2)}) %collective-permute-start.4) | collective-permute-done | bytes 1056 | tf_op jit(solution)/shard_map/ppermute | solution.py:19
  63.8 2.2 %collective-permute-start.2 = (bf16[128,512]{1,0:T(8,128)(2,1)S(1)}, bf16[128,512]{1,0:T(8,128)(2,1)S(1)}, u32[]{:S(2)}, u32[]{:S(2)}) collective-permute-start(bf16[128,512]{1,0:T(8,128)(2,1)S(1)} %bitcast.394), channel_id=1, source_target_pairs={{0,1},{1,2},{2,3},{3,4},{4,5},{5,6},{6,7},{7,8},{8,9},{9,10},{10,1... | collective-permute-start | bytes 393224 | tf_op jit(solution)/shard_map/ppermute | solution.py:19
  66.0 1.9 %collective-permute-start.1 = (bf16[128,512]{1,0:T(8,128)(2,1)S(1)}, bf16[128,512]{1,0:T(8,128)(2,1)S(1)}, u32[]{:S(2)}, u32[]{:S(2)}) collective-permute-start(bf16[128,512]{1,0:T(8,128)(2,1)S(1)} %bitcast.395), channel_id=1, source_target_pairs={{0,2},{1,3},{2,4},{3,5},{4,6},{5,7},{6,8},{7,9},{8,10},{9,11},{10,... | collective-permute-start | bytes 393224 | tf_op jit(solution)/shard_map/ppermute | solution.py:19
  68.0 2.2 %collective-permute-start = (bf16[128,512]{1,0:T(8,128)(2,1)S(1)}, bf16[128,512]{1,0:T(8,128)(2,1)S(1)}, u32[]{:S(2)}, u32[]{:S(2)}) collective-permute-start(bf16[128,512]{1,0:T(8,128)(2,1)S(1)} %bitcast.396), channel_id=1, source_target_pairs={{0,3},{1,4},{2,5},{3,6},{4,7},{5,8},{6,9},{7,10},{8,11},{9,12},{10... | collective-permute-start | bytes 393224 | tf_op jit(solution)/shard_map/ppermute | solution.py:19
  70.2 2.5 %collective-permute-start.8 = (bf16[128,512]{1,0:T(8,128)(2,1)S(1)}, bf16[128,512]{1,0:T(8,128)(2,1)S(1)}, u32[]{:S(2)}, u32[]{:S(2)}) collective-permute-start(bf16[128,512]{1,0:T(8,128)(2,1)S(1)} %bitcast.398), channel_id=1, source_target_pairs={{0,1},{1,2},{2,3},{3,4},{4,5},{5,6},{6,7},{7,8},{8,9},{9,10},{10,1... | collective-permute-start | bytes 393224 | tf_op jit(solution)/shard_map/ppermute | solution.py:19
  72.7 4.3 %collective-permute-start.7 = (bf16[128,512]{1,0:T(8,128)(2,1)S(1)}, bf16[128,512]{1,0:T(8,128)(2,1)S(1)}, u32[]{:S(2)}, u32[]{:S(2)}) collective-permute-start(bf16[128,512]{1,0:T(8,128)(2,1)S(1)} %bitcast.399), channel_id=1, source_target_pairs={{0,2},{1,3},{2,4},{3,5},{4,6},{5,7},{6,8},{7,9},{8,10},{9,11},{10,... | collective-permute-start | bytes 393224 | tf_op jit(solution)/shard_map/ppermute | solution.py:19
  77.0 2.0 %fusion.61 = (f32[]{:T(128)}, f32[]{:T(128)}, f32[]{:T(128)}, f32[]{:T(128)}) fusion(f32[7,2,128]{2,1,0:T(2,128)S(1)} %constant_dynamic-update-slice_fusion, f32[]{:T(128)} %bitcast.59, f32[]{:T(128)} %bitcast.60), kind=kLoop, calls=%fused_computation.132 | loop fusion | flops 8956 | bytes 7192 | tf_op jit(solution)/shard_map/reduce_sum | solution.py:53
  79.9 4.4 %broadcast_multiply_fusion = (f32[128]{0:T(128)S(1)}, f32[128]{0:T(128)S(1)}) fusion(f32[]{:T(128)} %get-tuple-element.18, f32[]{:T(128)} %get-tuple-element.16, f32[]{:T(128)} %get-tuple-element.17, f32[]{:T(128)} %get-tuple-element.15, f32[]{:T(128)} %get-tuple-element.20, f32[]{:T(128)} %get-tuple-element.19, s32[]{:T(128)} %bitcast.47, ...), kind=kLoop, calls=%fused_computation.156 | loop fusion | flops 1408 | bytes 1564 | tf_op jit(solution)/shard_map/mul | solution.py:116
  84.3 3.7 %fusion.70 = f32[1,128]{1,0:T(1,128)} fusion(f32[]{:T(128)} %get-tuple-element.18, f32[]{:T(128)} %get-tuple-element.16, f32[]{:T(128)} %get-tuple-element.17, f32[]{:T(128)} %get-tuple-element.15, s32[]{:T(128)} %bitcast.47, s32[1,128]{1,0:T(1,128)S(1)} %copy-done.14), kind=kLoop, calls=%fused_computation.154 | loop fusion | flops 640 | bytes 1044 | tf_op jit(solution)/shard_map/exp | solution.py:69
  88.0 7.5 %collective-permute-start.6 = (bf16[128,512]{1,0:T(8,128)(2,1)S(1)}, bf16[128,512]{1,0:T(8,128)(2,1)}, u32[]{:S(2)}, u32[]{:S(2)}) collective-permute-start(bf16[128,512]{1,0:T(8,128)(2,1)S(1)} %bitcast.400), channel_id=1, source_target_pairs={{0,3},{1,4},{2,5},{3,6},{4,7},{5,8},{6,9},{7,10},{8,11},{9,12},{10... | collective-permute-start | bytes 393224 | tf_op jit(solution)/shard_map/ppermute | solution.py:19
  96.3 1.7 fusion.91
  98.0 2.9 %convolution_bitcast_fusion.7 = f32[512,128]{0,1:T(8,128)} fusion(bf16[128,4,8,128]{0,3,2,1:T(8,128)(2,1)} %bitcast.386, f32[8,128]{1,0:T(8,128)S(1)} %get-tuple-element.50, pred[128,512]{0,1:T(8,128)(4,1)} %fusion.46, bf16[128,4,8,128]{0,3,2,1:T(8,128)(2,1)S(1)} %bitcast.375, bf16[512,512]{1,0:T(8,128)(2,1)} %pad_maximum_fusion.3), kind=kOutput, calls=%fused_computation.45 | convolution fusion | flops 271058432 | bytes 987136 | tf_op jit(solution)/shard_map/htj,thd->jd/dot_general | solution.py:114
  102.8 1.6 fusion.13
  106.5 2.1 %fusion.90 = (f32[8,128]{1,0:T(8,128)S(1)}, f32[8,128,512]{1,2,0:T(8,128)}) fusion(pred[128,512]{0,1:T(8,128)(4,1)S(1)} %copy-done.13, bf16[128,4,8,128]{0,3,2,1:T(8,128)(2,1)S(1)} %bitcast.377, bf16[512,512]{1,0:T(8,128)(2,1)S(1)} %copy-done.3), kind=kOutput, calls=%fused_computation.173 | convolution fusion | flops 136315392 | bytes 2560000 | tf_op jit(solution)/shard_map/sub | solution.py:98
  108.6 1.8 %convolution_bitcast_fusion.6 = f32[512,128]{0,1:T(8,128)} fusion(bf16[128,4,8,128]{0,3,2,1:T(8,128)(2,1)S(1)} %bitcast.392, f32[8,128]{1,0:T(8,128)S(1)} %get-tuple-element.46, pred[128,512]{0,1:T(8,128)(4,1)S(1)} %copy-done.13, bf16[128,4,8,128]{0,3,2,1:T(8,128)(2,1)S(1)} %bitcast.378, bf16[512,512]{1,0:T(8,128)(2,1)S(1)} %copy-done.3), kind=kOutput, calls=%fused_computation.44 | convolution fusion | flops 271058432 | bytes 987136 | tf_op jit(solution)/shard_map/htj,thd->jd/dot_general | solution.py:114
  110.4 2.2 %fusion.10 = (f32[8,128]{1,0:T(8,128)S(1)}, f32[512,128,8]{1,0,2:T(8,128)S(1)}) fusion(f32[8,128,512]{1,2,0:T(8,128)} %get-tuple-element.47, f32[8,128]{1,0:T(8,128)S(1)} %get-tuple-element.46, bf16[128,4,8,128]{0,3,2,1:T(8,128)(2,1)S(1)} %bitcast.393, bf16[512,512]{1,0:T(8,128)(2,1)} %copy-done.10), kind=kOutput, calls=%fused_computation.19 | convolution fusion | flops 136838144 | bytes 4595712 | tf_op jit(solution)/shard_map/thd,jd->htj/dot_general | solution.py:102
  114.6 2.1 %fusion.89 = (f32[8,128]{1,0:T(8,128)S(1)}, f32[8,128,512]{1,2,0:T(8,128)}) fusion(pred[128,512]{0,1:T(8,128)(4,1)S(1)} %copy-done.13, bf16[128,4,8,128]{0,3,2,1:T(8,128)(2,1)S(1)} %bitcast.380, bf16[512,512]{1,0:T(8,128)(2,1)S(1)} %copy-done.3), kind=kOutput, calls=%fused_computation.172 | convolution fusion | flops 136315392 | bytes 2560000 | tf_op jit(solution)/shard_map/sub | solution.py:98
  116.7 2.8 %convolution_bitcast_fusion.5 = f32[512,128]{0,1:T(8,128)} fusion(bf16[128,4,8,128]{0,3,2,1:T(8,128)(2,1)} %bitcast.388, f32[8,128]{1,0:T(8,128)S(1)} %get-tuple-element.42, pred[128,512]{0,1:T(8,128)(4,1)S(1)} %copy-done.13, bf16[128,4,8,128]{0,3,2,1:T(8,128)(2,1)S(1)} %bitcast.381, bf16[512,512]{1,0:T(8,128)(2,1)S(1)} %copy-done.3), kind=kOutput, calls=%fused_computation.43 | convolution fusion | flops 271058432 | bytes 987136 | tf_op jit(solution)/shard_map/htj,thd->jd/dot_general | solution.py:114
  119.5 2.3 %fusion.7 = (f32[8,128]{1,0:T(8,128)S(1)}, f32[512,128,8]{1,0,2:T(8,128)S(1)}) fusion(f32[8,128,512]{1,2,0:T(8,128)} %get-tuple-element.43, f32[8,128]{1,0:T(8,128)S(1)} %get-tuple-element.42, bf16[128,4,8,128]{0,3,2,1:T(8,128)(2,1)} %bitcast.389, bf16[512,512]{1,0:T(8,128)(2,1)} %copy-done.10), kind=kOutput, calls=%fused_computation.13 | convolution fusion | flops 136838144 | bytes 4595712 | tf_op jit(solution)/shard_map/thd,jd->htj/dot_general | solution.py:102
  123.7 2.1 %fusion.88 = (f32[8,128]{1,0:T(8,128)S(1)}, f32[8,128,512]{1,2,0:T(8,128)}) fusion(pred[128,512]{0,1:T(8,128)(4,1)S(1)} %copy-done.13, bf16[128,4,8,128]{0,3,2,1:T(8,128)(2,1)S(1)} %bitcast.383, bf16[512,512]{1,0:T(8,128)(2,1)S(1)} %copy-done.3), kind=kOutput, calls=%fused_computation.171 | convolution fusion | flops 136315392 | bytes 2560000 | tf_op jit(solution)/shard_map/sub | solution.py:98
  125.8 2.8 %convolution_bitcast_fusion.4 = f32[512,128]{0,1:T(8,128)} fusion(bf16[128,4,8,128]{0,3,2,1:T(8,128)(2,1)} %bitcast.390, f32[8,128]{1,0:T(8,128)S(1)} %get-tuple-element.38, pred[128,512]{0,1:T(8,128)(4,1)S(1)} %copy-done.13, bf16[128,4,8,128]{0,3,2,1:T(8,128)(2,1)S(1)} %bitcast.384, bf16[512,512]{1,0:T(8,128)(2,1)S(1)} %copy-done.3), kind=kOutput, calls=%fused_computation.42 | convolution fusion | flops 271058432 | bytes 987136 | tf_op jit(solution)/shard_map/htj,thd->jd/dot_general | solution.py:114
  128.7 1.2 fusion.78
  129.9 2.1 %pad_maximum_fusion.2 = f32[512,512]{0,1:T(8,128)} fusion(f32[512,128]{0,1:T(8,128)} %convolution_bitcast_fusion.4, f32[512,128]{0,1:T(8,128)} %convolution_bitcast_fusion.5, f32[512,128]{0,1:T(8,128)S(1)} %copy-done.9, f32[512,128]{0,1:T(8,128)S(1)} %copy-done.8), kind=kLoop, calls=%fused_computation.55 | loop fusion | flops 786432 | bytes 2097152 | tf_op jit(solution)/shard_map/concatenate | solution.py:121
  132.0 1.5 fusion.4
  135.4 2.2 %collective-permute-start.18 = (bf16[128,512]{0,1:T(8,128)(2,1)}, bf16[128,512]{0,1:T(8,128)(2,1)S(1)}, u32[]{:S(2)}, u32[]{:S(2)}) collective-permute-start(bf16[128,512]{0,1:T(8,128)(2,1)} %get-tuple-element.23), channel_id=1, source_target_pairs={{1,0},{2,1},{3,2},{4,3},{5,4},{6,5},{7,6},{8,7},{9,8},{10,9},{11,1... | collective-permute-start | bytes 393224 | tf_op jit(solution)/shard_map/ppermute | solution.py:19
  137.6 4.9 %collective-permute-start.20 = (bf16[128,512]{0,1:T(8,128)(2,1)}, bf16[128,512]{0,1:T(8,128)(2,1)S(1)}, u32[]{:S(2)}, u32[]{:S(2)}) collective-permute-start(bf16[128,512]{0,1:T(8,128)(2,1)} %get-tuple-element.24), channel_id=1, source_target_pairs={{3,0},{4,1},{5,2},{6,3},{7,4},{8,5},{9,6},{10,7},{11,8},{12,9},{13... | collective-permute-start | bytes 393224 | tf_op jit(solution)/shard_map/ppermute | solution.py:19
  142.5 7.5 %collective-permute-start.19 = (bf16[128,512]{0,1:T(8,128)(2,1)S(1)}, bf16[128,512]{0,1:T(8,128)(2,1)}, u32[]{:S(2)}, u32[]{:S(2)}) collective-permute-start(bf16[128,512]{0,1:T(8,128)(2,1)S(1)} %get-tuple-element.25), channel_id=1, source_target_pairs={{2,0},{3,1},{4,2},{5,3},{6,4},{7,5},{8,6},{9,7},{10,8},{11,9},{12,... | collective-permute-start | bytes 393224 | tf_op jit(solution)/shard_map/ppermute | solution.py:19
  150.0 1.5 pad_maximum_fusion
  151.5 1.9 %copy.59 = f32[1,128,4096]{2,1,0:T(8,128)S(1)} copy(f32[1,128,4096]{1,2,0:T(8,128)} %bitcast.373) | data formatting | bytes 4194304 | tf_op jit(solution)/shard_map/reshape | solution.py:118
  154.3 3.1 %collective-permute-start.15 = (bf16[128,512]{0,1:T(8,128)(2,1)}, bf16[128,512]{0,1:T(8,128)(2,1)}, u32[]{:S(2)}, u32[]{:S(2)}) collective-permute-start(bf16[128,512]{0,1:T(8,128)(2,1)} %get-tuple-element.26), channel_id=1, source_target_pairs={{1,0},{2,1},{3,2},{4,3},{5,4},{6,5},{7,6},{8,7},{9,8},{10,9},{11,1... | collective-permute-start | bytes 393224 | tf_op jit(solution)/shard_map/ppermute | solution.py:19
  157.4 2.9 %collective-permute-start.17 = (bf16[128,512]{0,1:T(8,128)(2,1)}, bf16[128,512]{0,1:T(8,128)(2,1)}, u32[]{:S(2)}, u32[]{:S(2)}) collective-permute-start(bf16[128,512]{0,1:T(8,128)(2,1)} %get-tuple-element.27), channel_id=1, source_target_pairs={{3,0},{4,1},{5,2},{6,3},{7,4},{8,5},{9,6},{10,7},{11,8},{12,9},{13... | collective-permute-start | bytes 393224 | tf_op jit(solution)/shard_map/ppermute | solution.py:19
  161.6 4.0 %collective-permute-start.16 = (bf16[128,512]{0,1:T(8,128)(2,1)}, bf16[128,512]{0,1:T(8,128)(2,1)S(1)}, u32[]{:S(2)}, u32[]{:S(2)}) collective-permute-start(bf16[128,512]{0,1:T(8,128)(2,1)} %get-tuple-element.28), channel_id=1, source_target_pairs={{2,0},{3,1},{4,2},{5,3},{6,4},{7,5},{8,6},{9,7},{10,8},{11,9},{12,... | collective-permute-start | bytes 393224 | tf_op jit(solution)/shard_map/ppermute | solution.py:19
  167.5 3.4 %collective-permute-done.17 = bf16[128,512]{0,1:T(8,128)(2,1)} collective-permute-done((bf16[128,512]{0,1:T(8,128)(2,1)}, bf16[128,512]{0,1:T(8,128)(2,1)}, u32[]{:S(2)}, u32[]{:S(2)}) %collective-permute-start.17) | collective-permute-done | bytes 131104 | tf_op jit(solution)/shard_map/ppermute | solution.py:19
  170.9 1.8 %collective-permute-done.16 = bf16[128,512]{0,1:T(8,128)(2,1)S(1)} collective-permute-done((bf16[128,512]{0,1:T(8,128)(2,1)}, bf16[128,512]{0,1:T(8,128)(2,1)S(1)}, u32[]{:S(2)}, u32[]{:S(2)}) %collective-permute-start.16) | collective-permute-done | bytes 131104 | tf_op jit(solution)/shard_map/ppermute | solution.py:19
  (91 shorter events, 20.7 us)
Async XLA Ops:
  0.6 41.6 %copy-start.6 = (bf16[1,128,4096]{2,1,0:T(8,128)(2,1)S(1)}, bf16[1,128,4096]{2,1,0:T(8,128)(2,1)}, u32[]{:S(2)}) copy-start(bf16[1,128,4096]{2,1,0:T(8,128)(2,1)} %param.12) | copy-start | bytes 3145732
  2.1 68.1 %collective-permute-start.13 = (f32[2,128]{1,0:T(2,128)S(1)}, f32[2,128]{1,0:T(2,128)S(1)}, u32[]{:S(2)}, u32[]{:S(2)}) collective-permute-start(f32[2,128]{1,0:T(2,128)S(1)} %get-tuple-element.29), channel_id=1, source_target_pairs={{2,0},{3,1},{4,2},{5,3},{6,4},{7,5},{8,6},{9,7},{10,8},{11,9},{12,... | collective-permute-start | bytes 3080 | tf_op jit(solution)/shard_map/ppermute | solution.py:19
  16.5 51.4 %collective-permute-start.12 = (f32[2,128]{1,0:T(2,128)S(1)}, f32[2,128]{1,0:T(2,128)S(1)}, u32[]{:S(2)}, u32[]{:S(2)}) collective-permute-start(f32[2,128]{1,0:T(2,128)S(1)} %get-tuple-element.29), channel_id=1, source_target_pairs={{1,0},{2,1},{3,2},{4,3},{5,4},{6,5},{7,6},{8,7},{9,8},{10,9},{11,1... | collective-permute-start | bytes 3080 | tf_op jit(solution)/shard_map/ppermute | solution.py:19
  19.0 53.7 %collective-permute-start.14 = (f32[2,128]{1,0:T(2,128)S(1)}, f32[2,128]{1,0:T(2,128)S(1)}, u32[]{:S(2)}, u32[]{:S(2)}) collective-permute-start(f32[2,128]{1,0:T(2,128)S(1)} %get-tuple-element.29), channel_id=1, source_target_pairs={{3,0},{4,1},{5,2},{6,3},{7,4},{8,5},{9,6},{10,7},{11,8},{12,9},{13... | collective-permute-start | bytes 3080 | tf_op jit(solution)/shard_map/ppermute | solution.py:19
  22.1 43.9 %collective-permute-start.5 = (f32[2,128]{1,0:T(2,128)S(1)}, f32[2,128]{1,0:T(2,128)S(1)}, u32[]{:S(2)}, u32[]{:S(2)}) collective-permute-start(f32[2,128]{1,0:T(2,128)S(1)} %get-tuple-element.29), channel_id=1, source_target_pairs={{0,1},{1,2},{2,3},{3,4},{4,5},{5,6},{6,7},{7,8},{8,9},{9,10},{10,1... | collective-permute-start | bytes 3080 | tf_op jit(solution)/shard_map/ppermute | solution.py:19
  26.9 3.1 %collective-permute-start.9 = (f32[48]{0:T(128)S(1)}, f32[48]{0:T(128)S(1)}, u32[]{:S(2)}, u32[]{:S(2)}) collective-permute-start(f32[48]{0:T(128)S(1)} %convolution_bitcast_fusion.13), channel_id=1, source_target_pairs={{0,96},{96,0},{192,288},{288,192},{384,480},{480,384},{576,672},{6... | collective-permute-start | bytes 584 | tf_op jit(solution)/shard_map/ppermute | solution.py:26
  30.0 5.5 %collective-permute-start.10 = (f32[48]{0:T(128)S(1)}, f32[48]{0:T(128)S(1)}, u32[]{:S(2)}, u32[]{:S(2)}) collective-permute-start(f32[48]{0:T(128)S(1)} %add.63), channel_id=1, source_target_pairs={{0,192},{96,288},{192,0},{288,96},{384,576},{480,672},{576,384},{6... | collective-permute-start | bytes 584 | tf_op jit(solution)/shard_map/ppermute | solution.py:26
  35.5 13.3 %copy-start.15 = (s32[1,48]{1,0:T(1,128)S(1)}, s32[1,48]{1,0:T(1,128)}, u32[]{:S(2)}) copy-start(s32[1,48]{1,0:T(1,128)} %param.14) | copy-start | bytes 580
  35.5 13.3 %copy-start.16 = (f32[1,48]{1,0:T(1,128)S(1)}, f32[1,48]{1,0:T(1,128)}, u32[]{:S(2)}) copy-start(f32[1,48]{1,0:T(1,128)} %param.15) | copy-start | bytes 580
  35.5 28.3 %copy-start.11 = (bf16[1,128,512]{2,1,0:T(8,128)(2,1)S(1)}, bf16[1,128,512]{2,1,0:T(8,128)(2,1)}, u32[]{:S(2)}) copy-start(bf16[1,128,512]{2,1,0:T(8,128)(2,1)} %param.10) | copy-start | bytes 393220
  35.5 34.7 %copy-start.12 = (bf16[1,128,512]{2,1,0:T(8,128)(2,1)S(1)}, bf16[1,128,512]{2,1,0:T(8,128)(2,1)}, u32[]{:S(2)}) copy-start(bf16[1,128,512]{2,1,0:T(8,128)(2,1)} %param.11) | copy-start | bytes 393220
  35.5 44.3 %copy-start.14 = (s32[1,128]{1,0:T(1,128)S(1)}, s32[1,128]{1,0:T(1,128)}, u32[]{:S(2)}) copy-start(s32[1,128]{1,0:T(1,128)} %param.13) | copy-start | bytes 1540
  35.5 8.0 %collective-permute-start.11 = (f32[48]{0:T(128)S(1)}, f32[48]{0:T(128)S(1)}, u32[]{:S(2)}, u32[]{:S(2)}) collective-permute-start(f32[48]{0:T(128)S(1)} %add.64), channel_id=1, source_target_pairs={{0,384},{96,480},{192,576},{288,672},{384,0},{480,96},{576,192},{6... | collective-permute-start | bytes 584 | tf_op jit(solution)/shard_map/ppermute | solution.py:26
  43.5 10.6 %collective-permute-start.3 = (f32[2,128]{1,0:T(2,128)S(1)}, f32[2,128]{1,0:T(2,128)S(1)}, u32[]{:S(2)}, u32[]{:S(2)}) collective-permute-start(f32[2,128]{1,0:T(2,128)S(1)} %get-tuple-element.29), channel_id=1, source_target_pairs={{0,3},{1,4},{2,5},{3,6},{4,7},{5,8},{6,9},{7,10},{8,11},{9,12},{10... | collective-permute-start | bytes 3080 | tf_op jit(solution)/shard_map/ppermute | solution.py:19
  54.1 9.7 %collective-permute-start.4 = (f32[2,128]{1,0:T(2,128)S(1)}, f32[2,128]{1,0:T(2,128)S(1)}, u32[]{:S(2)}, u32[]{:S(2)}) collective-permute-start(f32[2,128]{1,0:T(2,128)S(1)} %get-tuple-element.29), channel_id=1, source_target_pairs={{0,2},{1,3},{2,4},{3,5},{4,6},{5,7},{6,8},{7,9},{8,10},{9,11},{10,... | collective-permute-start | bytes 3080 | tf_op jit(solution)/shard_map/ppermute | solution.py:19
  63.8 24.1 %collective-permute-start.2 = (bf16[128,512]{1,0:T(8,128)(2,1)S(1)}, bf16[128,512]{1,0:T(8,128)(2,1)S(1)}, u32[]{:S(2)}, u32[]{:S(2)}) collective-permute-start(bf16[128,512]{1,0:T(8,128)(2,1)S(1)} %bitcast.394), channel_id=1, source_target_pairs={{0,1},{1,2},{2,3},{3,4},{4,5},{5,6},{6,7},{7,8},{8,9},{9,10},{10,1... | collective-permute-start | bytes 393224 | tf_op jit(solution)/shard_map/ppermute | solution.py:19
  66.0 29.5 %collective-permute-start.1 = (bf16[128,512]{1,0:T(8,128)(2,1)S(1)}, bf16[128,512]{1,0:T(8,128)(2,1)S(1)}, u32[]{:S(2)}, u32[]{:S(2)}) collective-permute-start(bf16[128,512]{1,0:T(8,128)(2,1)S(1)} %bitcast.395), channel_id=1, source_target_pairs={{0,2},{1,3},{2,4},{3,5},{4,6},{5,7},{6,8},{7,9},{8,10},{9,11},{10,... | collective-permute-start | bytes 393224 | tf_op jit(solution)/shard_map/ppermute | solution.py:19
  68.0 27.6 %collective-permute-start = (bf16[128,512]{1,0:T(8,128)(2,1)S(1)}, bf16[128,512]{1,0:T(8,128)(2,1)S(1)}, u32[]{:S(2)}, u32[]{:S(2)}) collective-permute-start(bf16[128,512]{1,0:T(8,128)(2,1)S(1)} %bitcast.396), channel_id=1, source_target_pairs={{0,3},{1,4},{2,5},{3,6},{4,7},{5,8},{6,9},{7,10},{8,11},{9,12},{10... | collective-permute-start | bytes 393224 | tf_op jit(solution)/shard_map/ppermute | solution.py:19
  70.2 30.7 %collective-permute-start.8 = (bf16[128,512]{1,0:T(8,128)(2,1)S(1)}, bf16[128,512]{1,0:T(8,128)(2,1)S(1)}, u32[]{:S(2)}, u32[]{:S(2)}) collective-permute-start(bf16[128,512]{1,0:T(8,128)(2,1)S(1)} %bitcast.398), channel_id=1, source_target_pairs={{0,1},{1,2},{2,3},{3,4},{4,5},{5,6},{6,7},{7,8},{8,9},{9,10},{10,1... | collective-permute-start | bytes 393224 | tf_op jit(solution)/shard_map/ppermute | solution.py:19
  72.7 28.2 %collective-permute-start.7 = (bf16[128,512]{1,0:T(8,128)(2,1)S(1)}, bf16[128,512]{1,0:T(8,128)(2,1)S(1)}, u32[]{:S(2)}, u32[]{:S(2)}) collective-permute-start(bf16[128,512]{1,0:T(8,128)(2,1)S(1)} %bitcast.399), channel_id=1, source_target_pairs={{0,2},{1,3},{2,4},{3,5},{4,6},{5,7},{6,8},{7,9},{8,10},{9,11},{10,... | collective-permute-start | bytes 393224 | tf_op jit(solution)/shard_map/ppermute | solution.py:19
  88.0 13.9 %collective-permute-start.6 = (bf16[128,512]{1,0:T(8,128)(2,1)S(1)}, bf16[128,512]{1,0:T(8,128)(2,1)}, u32[]{:S(2)}, u32[]{:S(2)}) collective-permute-start(bf16[128,512]{1,0:T(8,128)(2,1)S(1)} %bitcast.400), channel_id=1, source_target_pairs={{0,3},{1,4},{2,5},{3,6},{4,7},{5,8},{6,9},{7,10},{8,11},{9,12},{10... | collective-permute-start | bytes 393224 | tf_op jit(solution)/shard_map/ppermute | solution.py:19
  102.8 1.6 copy-start.10
  104.7 1.7 %copy-start.3 = (bf16[512,512]{1,0:T(8,128)(2,1)S(1)}, bf16[512,512]{1,0:T(8,128)(2,1)}, u32[]{:S(2)}) copy-start(bf16[512,512]{1,0:T(8,128)(2,1)} %pad_maximum_fusion.3) | copy-start | bytes 1572868
  104.7 1.7 %copy-start.13 = (pred[128,512]{0,1:T(8,128)(4,1)S(1)}, pred[128,512]{0,1:T(8,128)(4,1)}, u32[]{:S(2)}) copy-start(pred[128,512]{0,1:T(8,128)(4,1)} %fusion.46) | copy-start | bytes 196612
  106.5 2.1 %copy-start.7 = (bf16[1,128,4096]{1,2,0:T(8,128)(2,1)S(1)}, bf16[1,128,4096]{1,2,0:T(8,128)(2,1)}, u32[]{:S(2)}) copy-start(bf16[1,128,4096]{1,2,0:T(8,128)(2,1)} %copy.43) | copy-start | bytes 3145732
  110.4 2.3 %copy-start.1 = (f32[8,128,512]{1,2,0:T(8,128)S(1)}, f32[8,128,512]{1,2,0:T(8,128)}, u32[]{:S(2)}) copy-start(f32[8,128,512]{1,2,0:T(8,128)} %get-tuple-element.47) | copy-start | bytes 6291460
  119.5 2.4 %copy-start.2 = (f32[8,128,512]{1,2,0:T(8,128)S(1)}, f32[8,128,512]{1,2,0:T(8,128)}, u32[]{:S(2)}) copy-start(f32[8,128,512]{1,2,0:T(8,128)} %get-tuple-element.43) | copy-start | bytes 6291460
  125.8 2.9 %copy-start.8 = (f32[512,128]{0,1:T(8,128)S(1)}, f32[512,128]{0,1:T(8,128)}, u32[]{:S(2)}) copy-start(f32[512,128]{0,1:T(8,128)} %convolution_bitcast_fusion.7) | copy-start | bytes 786436
  125.8 2.9 %copy-start.9 = (f32[512,128]{0,1:T(8,128)S(1)}, f32[512,128]{0,1:T(8,128)}, u32[]{:S(2)}) copy-start(f32[512,128]{0,1:T(8,128)} %convolution_bitcast_fusion.6) | copy-start | bytes 786436
  128.7 3.3 %copy-start = (f32[8,128,512]{1,2,0:T(8,128)S(1)}, f32[8,128,512]{1,2,0:T(8,128)}, u32[]{:S(2)}) copy-start(f32[8,128,512]{1,2,0:T(8,128)} %get-tuple-element.39) | copy-start | bytes 6291460
  133.8 16.2 %copy-start.4 = (f32[128,1,8,128]{0,3,2,1:T(8,128)S(1)}, f32[128,1,8,128]{0,3,2,1:T(8,128)}, u32[]{:S(2)}) copy-start(f32[128,1,8,128]{0,3,2,1:T(8,128)} %convolution_bitcast_fusion.2) | copy-start | bytes 1572868
  133.8 16.2 %copy-start.5 = (f32[128,1,8,128]{0,3,2,1:T(8,128)S(1)}, f32[128,1,8,128]{0,3,2,1:T(8,128)}, u32[]{:S(2)}) copy-start(f32[128,1,8,128]{0,3,2,1:T(8,128)} %convolution_bitcast_fusion.1) | copy-start | bytes 1572868
  135.4 26.2 %collective-permute-start.18 = (bf16[128,512]{0,1:T(8,128)(2,1)}, bf16[128,512]{0,1:T(8,128)(2,1)S(1)}, u32[]{:S(2)}, u32[]{:S(2)}) collective-permute-start(bf16[128,512]{0,1:T(8,128)(2,1)} %get-tuple-element.23), channel_id=1, source_target_pairs={{1,0},{2,1},{3,2},{4,3},{5,4},{6,5},{7,6},{8,7},{9,8},{10,9},{11,1... | collective-permute-start | bytes 393224 | tf_op jit(solution)/shard_map/ppermute | solution.py:19
  137.6 28.0 %collective-permute-start.20 = (bf16[128,512]{0,1:T(8,128)(2,1)}, bf16[128,512]{0,1:T(8,128)(2,1)S(1)}, u32[]{:S(2)}, u32[]{:S(2)}) collective-permute-start(bf16[128,512]{0,1:T(8,128)(2,1)} %get-tuple-element.24), channel_id=1, source_target_pairs={{3,0},{4,1},{5,2},{6,3},{7,4},{8,5},{9,6},{10,7},{11,8},{12,9},{13... | collective-permute-start | bytes 393224 | tf_op jit(solution)/shard_map/ppermute | solution.py:19
  142.5 23.1 %collective-permute-start.19 = (bf16[128,512]{0,1:T(8,128)(2,1)S(1)}, bf16[128,512]{0,1:T(8,128)(2,1)}, u32[]{:S(2)}, u32[]{:S(2)}) collective-permute-start(bf16[128,512]{0,1:T(8,128)(2,1)S(1)} %get-tuple-element.25), channel_id=1, source_target_pairs={{2,0},{3,1},{4,2},{5,3},{6,4},{7,5},{8,6},{9,7},{10,8},{11,9},{12,... | collective-permute-start | bytes 393224 | tf_op jit(solution)/shard_map/ppermute | solution.py:19
  154.3 13.2 %collective-permute-start.15 = (bf16[128,512]{0,1:T(8,128)(2,1)}, bf16[128,512]{0,1:T(8,128)(2,1)}, u32[]{:S(2)}, u32[]{:S(2)}) collective-permute-start(bf16[128,512]{0,1:T(8,128)(2,1)} %get-tuple-element.26), channel_id=1, source_target_pairs={{1,0},{2,1},{3,2},{4,3},{5,4},{6,5},{7,6},{8,7},{9,8},{10,9},{11,1... | collective-permute-start | bytes 393224 | tf_op jit(solution)/shard_map/ppermute | solution.py:19
  157.4 13.5 %collective-permute-start.17 = (bf16[128,512]{0,1:T(8,128)(2,1)}, bf16[128,512]{0,1:T(8,128)(2,1)}, u32[]{:S(2)}, u32[]{:S(2)}) collective-permute-start(bf16[128,512]{0,1:T(8,128)(2,1)} %get-tuple-element.27), channel_id=1, source_target_pairs={{3,0},{4,1},{5,2},{6,3},{7,4},{8,5},{9,6},{10,7},{11,8},{12,9},{13... | collective-permute-start | bytes 393224 | tf_op jit(solution)/shard_map/ppermute | solution.py:19
  161.6 11.2 %collective-permute-start.16 = (bf16[128,512]{0,1:T(8,128)(2,1)}, bf16[128,512]{0,1:T(8,128)(2,1)S(1)}, u32[]{:S(2)}, u32[]{:S(2)}) collective-permute-start(bf16[128,512]{0,1:T(8,128)(2,1)} %get-tuple-element.28), channel_id=1, source_target_pairs={{2,0},{3,1},{4,2},{5,3},{6,4},{7,5},{8,6},{9,7},{10,8},{11,9},{12,... | collective-permute-start | bytes 393224 | tf_op jit(solution)/shard_map/ppermute | solution.py:19

commit v2 on v1

v2 whole, which is shorter than its diff:
```python
import functools
import math

import jax
import jax.numpy as jnp
from jax import lax
from jax.experimental import pallas as pl
from jax.experimental.pallas import tpu as pltpu
from jax.sharding import PartitionSpec as P

QHEADS = 32
KVHEADS = 4
HEAD_DIM = 128
SPAN = 3
GROUP = 8
MEAN_LEN = 256
GROUP_HEADS = QHEADS // KVHEADS
INFO_ROWS = 16
CORES = 2
CHUNKS = 2
CHUNK_HEADS = KVHEADS // CHUNKS
PAIR = 2 * HEAD_DIM
SCORE_SCALE = 1.0 / math.sqrt(HEAD_DIM)
HIDDEN = -1e30


def passed_along(array, axis, by, around=False):
    count = lax.axis_size(axis)
    pairs = [(i, (i + by) % count) for i in range(count) if around or 0 <= i + by < count]
    return lax.ppermute(array, axis, pairs)


def from_other_core(array):
    return lax.ppermute(array, "dp", [(i, i ^ CORES - 1) for i in range(lax.axis_size("dp"))])


def turn(at, chips):
    return 1 + at % (chips - 1)


def from_turned(array):
    ranks, count = lax.axis_size("dp"), lax.axis_size("ctx")
    chips = ranks // CORES
    if chips == 1:
        return jnp.zeros_like(array)
    pairs = [
        ((rank + turn(at, chips) * CORES) % ranks * count + at, rank * count + at)
        for rank in range(ranks)
        for at in range(count)
    ]
    return lax.ppermute(array, ("dp", "ctx"), pairs)


def forward(packed, sums):
    came = []
    first, second = packed
    turned = None
    for hop in range(SPAN):
        first = passed_along(first, "ctx", 1)
        second = passed_along(second, "ctx", 1)
        if hop == 0:
            sums = sums + from_other_core(sums)
            first, sums = lax.optimization_barrier((first, sums))
        if hop == 1:
            turned = from_turned(sums)
            first, turned = lax.optimization_barrier((first, turned))
        came.append([first, second])
    return came, sums, turned


def eye(size):
    rows = lax.broadcasted_iota(jnp.int32, (size, size), 0)
    return rows == lax.broadcasted_iota(jnp.int32, (size, size), 1)


def sample_hot(sample_ids, groups):
    shape = (groups, sample_ids.shape[1])
    return lax.broadcasted_iota(jnp.int32, shape, 0) == sample_ids


def with_lines(info, first, line):
    high = line.astype(jnp.bfloat16).astype(jnp.float32)
    middle = (line - high).astype(jnp.bfloat16).astype(jnp.float32)
    at = lax.broadcasted_iota(jnp.int32, info.shape, 0)
    for k, part in enumerate((high, middle, line - high - middle)):
        info = jnp.where(at == first + k, part, info)
    return info


def line_of(block, first):
    return block[first : first + 1] + block[first + 1 : first + 2] + block[first + 2 : first + 3]


def pack_body(keys, values, ids, new_logp, old_logp, sample_ids, rewards, *outs):
    *packed, sums = outs
    rows = keys.shape[0]
    log_ratio = new_logp[...] - old_logp[...]
    at = lax.broadcasted_iota(jnp.int32, (INFO_ROWS, rows), 0)
    info = jnp.where(at == 0, (ids[...] + 1).astype(jnp.float32), 0.0)
    info = with_lines(info, 1, log_ratio).astype(jnp.bfloat16)
    for head in range(KVHEADS):
        columns = slice(head * HEAD_DIM, (head + 1) * HEAD_DIM)
        out = packed[head // CHUNK_HEADS]
        at = 2 * (head % CHUNK_HEADS) * rows
        out[at : at + rows, :] = keys[:, columns]
        out[at + rows : at + 2 * rows, :] = values[:, columns]
    packed[0][2 * CHUNK_HEADS * rows :, :] = info
    groups = sums.shape[1]
    hot = sample_hot(sample_ids[...], groups)
    column = jnp.sum(jnp.where(hot, rewards[...], 0.0), axis=1, keepdims=True)
    sums[...] = jnp.sum(jnp.where(eye(groups), column, 0.0), axis=0, keepdims=True)


def over_lanes(ref):
    return ref[0:1, :].astype(jnp.float32)


def advantage_of(sums, turned, others, sample_ids, rewards):
    chips = lax.axis_size("dp") // CORES
    chip = lax.axis_index("dp") // CORES
    at = lax.axis_index("ctx")
    held = [(chip, sums[...])]
    if chips > 1:
        lines = [turned[...]] + [line_of(block, 4) for block in others[: chips - 2]]
        held += [((chip + turn(at + k, chips)) % chips, line) for k, line in enumerate(lines)]
    total = jnp.zeros_like(sums)
    for wanted in range(chips):
        for source, line in held:
            total = total + jnp.where(source == wanted, line, 0.0)
    hot = sample_hot(sample_ids[...], sums.shape[1])
    column = jnp.sum(jnp.where(eye(sums.shape[1]), total, 0.0), axis=1, keepdims=True)
    return rewards[...] - jnp.sum(jnp.where(hot, column, 0.0), axis=0, keepdims=True) / GROUP


def attention_body(chunk, q_ref, g_ref, own_info, own, came1, came2, came3, *rest):
    rows = q_ref.shape[0]
    step = pl.program_id(0)
    infos = [ref.at[2 * CHUNK_HEADS * rows :, :] for ref in (came1, came2, came3)]
    came = (came1, came2, came3)
    if chunk:
        came, rest = rest[:3], rest[3:]
    else:
        turned, rest = rest[0], rest[1:]
    dq_ref, sum0, sum1, sum2, sum3 = rest
    out_rows = pl.ds(pl.multiple_of(step * 2 * rows, 2 * rows), 2 * rows)
    pairs = [own[...]] + [ref[out_rows, :] for ref in came]
    own_ids = over_lanes(own_info)
    first = own_ids[:, 0:1]

    def count(ids):
        return jnp.sum((ids == first).astype(jnp.float32), axis=1, keepdims=True)

    head_count = count(own_ids).astype(jnp.int32)
    below = sum(count(over_lanes(ref)) for ref in infos).astype(jnp.int32)
    key_at = lax.broadcasted_iota(jnp.int32, (rows, rows), 0)
    query_at = lax.broadcasted_iota(jnp.int32, (rows, rows), 1)
    near = key_at <= query_at
    start = jnp.where(query_at < head_count, -below, head_count)

    def bias(at):
        return jnp.where(at >= start, 0.0, HIDDEN)

    hidden = jnp.concatenate(
        [
            bias(jnp.where(near, key_at, key_at - SPAN * rows)),
            bias(key_at - rows),
            bias(key_at - 2 * rows),
        ],
        axis=0,
    )
    pairs = [pairs[3], pairs[0], pairs[1], pairs[2]]
    key_rows = jnp.concatenate([pair[:rows] for pair in pairs], axis=0)
    value_rows = jnp.concatenate([pair[rows:] for pair in pairs], axis=0)

    def stacked(ref):
        return jnp.concatenate(
            [ref[:, h * HEAD_DIM : (h + 1) * HEAD_DIM] for h in range(GROUP_HEADS)], axis=0
        )

    def merged(tall):
        return jnp.concatenate(
            [jnp.where(near, tall[rows : 2 * rows], tall[:rows]), tall[2 * rows :]], axis=0
        )

    def parted(short):
        blank = jnp.zeros((rows, rows), jnp.bfloat16)
        return jnp.concatenate(
            [
                jnp.where(near, blank, short[:rows]),
                jnp.where(near, short[:rows], blank),
                short[rows:],
            ],
            axis=0,
        )

    query_rows = stacked(q_ref)
    grad_rows = stacked(g_ref)
    minor = (((1,), (1,)), ((), ()))
    scores = lax.dot_general(key_rows, query_rows, minor, preferred_element_type=jnp.float32)
    dprob = lax.dot_general(value_rows, grad_rows, minor, preferred_element_type=jnp.float32)
    to_power = SCORE_SCALE * math.log2(math.e)
    weight_parts = []
    dscore_parts = []
    for h in range(GROUP_HEADS):
        lanes = slice(h * rows, (h + 1) * rows)
        part = merged(scores[:, lanes]) + hidden
        top = jnp.max(part, axis=0, keepdims=True)
        powers = jnp.exp2((part - top) * to_power)
        weights = powers * (1.0 / jnp.sum(powers, axis=0, keepdims=True))
        grads = merged(dprob[:, lanes])
        delta = jnp.sum(weights * grads, axis=0, keepdims=True)
        weight_parts.append(parted(weights.astype(jnp.bfloat16)))
        dscore_parts.append(parted((weights * (grads - delta)).astype(jnp.bfloat16)))
    weights_bf = jnp.concatenate(weight_parts, axis=1)
    dscore = jnp.concatenate(dscore_parts, axis=1)
    value_part = jnp.dot(weights_bf, grad_rows, preferred_element_type=jnp.float32)
    key_part = jnp.dot(dscore, query_rows, preferred_element_type=jnp.float32)
    query_part = jnp.dot(key_rows.T, dscore, preferred_element_type=jnp.float32)
    for h in range(GROUP_HEADS):
        lanes = slice(h * rows, (h + 1) * rows)
        dq_ref[:, h * HEAD_DIM : (h + 1) * HEAD_DIM] = query_part[:, lanes].T.astype(jnp.bfloat16)
    for at, out in enumerate((sum3, sum0, sum1, sum2)):
        lines = slice(at * rows, (at + 1) * rows)
        at_rows = slice(None) if out is sum0 else out_rows
        out[at_rows, :] = jnp.concatenate(
            [key_part[lines].astype(out.dtype), value_part[lines].astype(out.dtype)], axis=0
        )
    if not chunk:
        base = 2 * CHUNK_HEADS * rows
        sum3[base:, :] = with_lines(own_info[...].astype(jnp.float32), 4, turned[...]).astype(
            sum3.dtype
        )
        for out in (sum2, sum1):
            out[base:, :] = jnp.zeros((INFO_ROWS, HEAD_DIM), out.dtype)


def weights_of(own_info, blocks, advantage):
    rows = own_info.shape[1]
    own_ids = over_lanes(own_info)
    first = own_ids[:, 0:1]
    last = own_ids[:, rows - 1 : rows]
    resp_at = (lax.broadcasted_iota(jnp.int32, advantage.shape, 1) + 1).astype(jnp.float32)
    logs = [line_of(block, 1) for block in blocks]

    def of_response(wanted):
        totals = jnp.zeros((1, rows), jnp.float32)
        counts = jnp.zeros((1, rows), jnp.float32)
        for block, log in zip(blocks, logs):
            same = block[0:1] == wanted
            totals = totals + jnp.where(same, log, 0.0)
            counts = counts + jnp.where(same, 1.0, 0.0)
        total = jnp.sum(totals, axis=1, keepdims=True)
        length = jnp.sum(counts, axis=1, keepdims=True)
        gain = jnp.sum(jnp.where(resp_at == wanted, advantage, 0.0), axis=1, keepdims=True)
        ratio = jnp.exp(total / length)
        return ratio, -gain * ratio * MEAN_LEN / length

    first_ratio, first_weight = of_response(first)
    last_ratio, last_weight = of_response(last)
    head_count = jnp.sum((own_ids == first).astype(jnp.float32), axis=1, keepdims=True)
    row_at = lax.broadcasted_iota(jnp.int32, (rows, 1), 0)
    weight = jnp.where(row_at < head_count.astype(jnp.int32), first_weight, last_weight)
    return jnp.where(own_ids == first, first_ratio, last_ratio), weight


def write_kv(weight, sum0, came, dk_out, dv_out):
    rows = dk_out.shape[0]
    for head in range(CHUNK_HEADS):
        columns = slice(head * HEAD_DIM, (head + 1) * HEAD_DIM)
        for at, out, scale in ((0, dk_out, weight * SCORE_SCALE), (1, dv_out, weight)):
            lines = slice((2 * head + at) * rows, (2 * head + at + 1) * rows)
            whole = sum0[lines, :] + came[lines, :].astype(jnp.float32)
            out[:, columns] = (whole * scale).astype(jnp.bfloat16)


def on_chip(array):
    return pltpu.with_memory_space_constraint(array, pltpu.VMEM)


def final_body(own_info, *refs):
    came, back = refs[:3], refs[3:6]
    sums, turned, sample_ids, rewards, sum0 = refs[6:11]
    parts = refs[11:-6]
    dq_out, dk_out, dv_out, ratio_out, weight_out, advantage_out = refs[-6:]
    base = sum0.shape[0]
    blocks = [own_info[...].astype(jnp.float32)]
    blocks += [ref[base:, :].astype(jnp.float32) for ref in (*came, *back)]
    advantage = advantage_of(sums, turned, blocks[SPAN + 1 :], sample_ids, rewards)
    advantage_out[...] = advantage
    ratio_out[...], weight = weights_of(own_info, blocks, advantage)
    weight_out[...] = jnp.broadcast_to(weight, weight_out.shape)
    scaled = weight * SCORE_SCALE
    left = 0
    for part in parts:
        right = left + part.shape[1]
        dq_out[:, left:right] = (part[...].astype(jnp.float32) * scaled).astype(jnp.bfloat16)
        left = right
    write_kv(weight, sum0, back[2], dk_out, dv_out)


def rest_body(weight, sum0, came, dk_in, dv_in, dk_out, dv_out):
    del dk_in, dv_in
    write_kv(weight[:, 0:1], sum0, came, dk_out, dv_out)


def shards(queries, keys, values, logp_grad, response_ids, sample_ids, rewards, new_logp, old_logp):
    rows = queries.shape[1]
    resp_count = rewards.shape[1]
    group_width = GROUP_HEADS * HEAD_DIM
    kv_width = CHUNK_HEADS * HEAD_DIM
    bf = jnp.bfloat16
    height = 2 * CHUNK_HEADS * rows
    talls = [height if c else height + INFO_ROWS for c in range(CHUNKS)]
    *packed, sums = pl.pallas_call(
        pack_body,
        out_shape=[
            *[jax.ShapeDtypeStruct((tall, HEAD_DIM), bf) for tall in talls],
            jax.ShapeDtypeStruct((1, HEAD_DIM), jnp.float32),
        ],
        name="pack",
    )(keys[0], values[0], response_ids, new_logp, old_logp, sample_ids, rewards)
    came, sums, turned = forward(packed, sums)
    came = [[on_chip(piece) for piece in pieces] for pieces in came]
    info_spec = pl.BlockSpec((INFO_ROWS, HEAD_DIM), lambda g: (height // INFO_ROWS, 0))
    chip_spec = pl.BlockSpec(memory_space=pltpu.VMEM)
    line_spec = pl.BlockSpec((1, HEAD_DIM), lambda g: (0, 0))
    resp = pl.BlockSpec((1, resp_count), lambda g: (0, 0))
    parts = []
    for c in range(CHUNKS):
        head_spec = pl.BlockSpec((rows, group_width), lambda g, c=c: (0, g + c * CHUNK_HEADS))
        own_spec = pl.BlockSpec((2 * rows, HEAD_DIM), lambda g: (g, 0))
        more_specs, more = [line_spec], [turned]
        if c:
            more_specs, more = [chip_spec] * 3, [pieces[c] for pieces in came]
        parts.append(
            pl.pallas_call(
                functools.partial(attention_body, c),
                grid=(CHUNK_HEADS,),
                in_specs=[head_spec, head_spec, info_spec, own_spec]
                + [chip_spec] * 3
                + more_specs,
                out_specs=[
                    pl.BlockSpec((rows, group_width), lambda g: (0, g)),
                    pl.BlockSpec((2 * rows, HEAD_DIM), lambda g: (g, 0)),
                ]
                + [chip_spec] * 3,
                out_shape=[
                    jax.ShapeDtypeStruct((rows, CHUNK_HEADS * group_width), bf),
                    jax.ShapeDtypeStruct((height, HEAD_DIM), jnp.float32),
                ]
                + [pltpu.VMEM((talls[c], HEAD_DIM), bf)] * 3,
                name=f"attention{c}",
            )(queries[0], logp_grad[0], packed[0], packed[c], *[pieces[0] for pieces in came], *more)
        )
    back = []
    at = [part[4] for part in parts]
    for hop in range(SPAN):
        at = [passed_along(piece, "ctx", -1, around=c == 0) for c, piece in enumerate(at)]
        back.append(on_chip(at[0]))
        if hop < SPAN - 1:
            at = [piece + part[3 - hop] for piece, part in zip(at, parts)]

    def whole(shape, at=(0, 0)):
        return pl.BlockSpec(shape, lambda g: at)

    query_grad, key_grad, value_grad, token_ratio, weight, advantage = pl.pallas_call(
        final_body,
        grid=(1,),
        in_specs=[info_spec]
        + [chip_spec] * 6
        + [line_spec, line_spec, resp, resp, whole((height, HEAD_DIM))]
        + [whole((rows, CHUNK_HEADS * group_width))] * CHUNKS,
        out_specs=[
            whole((rows, queries.shape[2])),
            whole((rows, kv_width)),
            whole((rows, kv_width)),
            whole((1, rows)),
            whole((rows, HEAD_DIM)),
            resp,
        ],
        out_shape=[
            jax.ShapeDtypeStruct((rows, queries.shape[2]), bf),
            jax.ShapeDtypeStruct((rows, keys.shape[2]), bf),
            jax.ShapeDtypeStruct((rows, keys.shape[2]), bf),
            jax.ShapeDtypeStruct((1, rows), jnp.float32),
            jax.ShapeDtypeStruct((rows, HEAD_DIM), jnp.float32),
            jax.ShapeDtypeStruct((1, resp_count), jnp.float32),
        ],
        name="final",
    )(packed[0], *[pieces[0] for pieces in came], *back, sums, turned, sample_ids,
      rewards, parts[0][1], *[part[0] for part in parts])
    kv_spec = whole((rows, kv_width), (0, 1))
    any_spec = pl.BlockSpec(memory_space=pl.ANY)
    key_grad, value_grad = pl.pallas_call(
        rest_body,
        grid=(1,),
        in_specs=[
            whole((rows, HEAD_DIM)),
            whole((height, HEAD_DIM)),
            chip_spec,
            any_spec,
            any_spec,
        ],
        out_specs=[kv_spec, kv_spec],
        out_shape=[jax.ShapeDtypeStruct((rows, keys.shape[2]), bf)] * 2,
        input_output_aliases={3: 0, 4: 1},
        name="rest",
    )(weight, parts[1][1], on_chip(at[1]), key_grad, value_grad)
    return (query_grad[None], key_grad[None], value_grad[None], token_ratio, advantage)


def solution(mesh):
    return jax.shard_map(
        shards,
        mesh=mesh,
        in_specs=(
            P("dp", "ctx", None),
            P("dp", "ctx", None),
            P("dp", "ctx", None),
            P("dp", "ctx", None),
            P("dp", "ctx"),
            P("dp", None),
            P("dp", None),
            P("dp", "ctx"),
            P("dp", "ctx"),
        ),
        out_specs=(
            P("dp", "ctx", None),
            P("dp", "ctx", None),
            P("dp", "ctx", None),
            P("dp", "ctx"),
            P("dp", None),
        ),
        check_vma=False,
    )
```

time: 176 us -> 87.1 us (0.49)
  starting transfers between devices: 87.8 us -> 49.8 us
  matrix products: 35.1 us -> 0 us
  other arithmetic: 23.6 us -> 0.16 us
  Pallas kernels: 0 us -> 17.5 us
  local copies, waits for them, and re-layouts: 9.29 us -> 0.01 us
    ppermute x18 -> x12, starting transfers between devices: 77.4 us -> 43.2 us  [passed_along(): return lax.ppermute(array, axis, pairs)]
    dot_general x18 -> x0, matrix products: 27.2 us -> none  [the longest x4 10.3 us: shards(): jnp.einsum('htj,thd->jd', weights_bf, grad_group, preferred_element_type=...]
    pallas_call x0 -> x5, Pallas kernels: none -> 17.5 us  [the longest x2 11 us: shards(): pl.pallas_call(functools.partial(attention_body, c), grid=(CHUNK_HEADS,),...]
    sub x4 -> x0, matrix products: 7.93 us -> none  [shards(): powers = jnp.exp(scores - row_top)]
    unnamed x43 -> x6, local copies, waits for them, and re-layouts: 4.66 us -> 0.01 us
    mul x1 -> x0, other arithmetic: 4.39 us -> none  [shards(): scaled_weight = (tok_weight * score_scale)[:, None]]
    concatenate x4 -> x0, other arithmetic: 3.92 us -> none  [the longest x1 2.08 us: shards(): value_full = jnp.concatenate(value_parts, axis=1)]
    ppermute x3 -> x2, starting transfers between devices: 10.4 us -> 6.59 us  [the longest x1 4.67 us: from_turned(): return lax.ppermute(array, ('dp', 'ctx'), pairs)]
  transfers between devices with their start and end apart: 21 -> 14, of which waited for: 6 -> 7; matrix products, arithmetic and copies ran while one was open for 18% -> 0% of each run, Pallas kernels for 0% -> 16%
where the time goes in v2:
time: 87.1 us; the launch traced here: 86.6 us
  starting transfers between devices  49.8 us (57%)
  waiting for transfers between devices  18.3 us (21%)
  Pallas kernels  17.5 us (20%)
    ppermute x12, starting transfers between devices, passed_along(): return lax.ppermute(array, axis, pairs)  43.2 us
    ppermute x12, waiting for transfers between devices, passed_along(): return lax.ppermute(array, axis, pairs)  15.9 us
    pallas_call x2, Pallas kernels, shards(): pl.pallas_call(functools.partial(attention_body, c), grid=(CHUNK_HEADS,),...  11 us
    ppermute x1, starting transfers between devices, from_turned(): return lax.ppermute(array, ('dp', 'ctx'), pairs)  4.67 us
    pallas_call x1, Pallas kernels, shards(): pl.pallas_call(final_body, grid=(1,), in_specs=[info_spec] + [chip_spec]...  2.99 us
    ppermute x1, starting transfers between devices, from_other_core(): lax.ppermute(array, 'dp', [(i, i ^ CORES - 1) for i in range(lax.axis_siz...  1.92 us
    pallas_call x1, Pallas kernels, shards(): pl.pallas_call(pack_body, out_shape=[*[jax.ShapeDtypeStruct((tall, HEAD_D...  1.74 us
  transfers between devices with their start and end apart: 14, of which 7 were waited for; matrix products, arithmetic and copies ran while one was open for 0% of the time, Pallas kernels for 16%

profile of v2, /device:TPU:32, one launch (start us, length us, event | category | flops | bytes accessed | tf_op | source)
XLA Modules:
  0.0 86.6 jit_solution(9900734357676515477)
XLA Ops:
  0.6 1.7 %pack.1 = (bf16[528,128]{1,0:T(8,128)(2,1)}, bf16[512,128]{1,0:T(8,128)(2,1)}, f32[1,128]{1,0:T(1,128)}) custom-call(bf16[128,512]{1,0:T(8,128)(2,1)} %bitcast.11, bf16[128,512]{1,0:T(8,128)(2,1)} %bitcast.12, s32[1,128]{1,0:T(1,128)} %ids.1, f32[1,128]{1,0:T(1,128)} %new_logp.1, f32[1,128]{1,0:T(1,128)} %old_logp.1, s32[1,48]{1,0:T(1,128)} %refs_8_.1, ...), custom_call_target="tpu_custom_call" | custom-call | tf_op jit(solution)/shard_map/pack/pallas_call | solution.py:314
  2.4 4.3 %collective-permute-start = (bf16[528,128]{1,0:T(8,128)(2,1)}, bf16[528,128]{1,0:T(8,128)(2,1)S(1)}, u32[]{:S(2)}, u32[]{:S(2)}) collective-permute-start(bf16[528,128]{1,0:T(8,128)(2,1)} %get-tuple-element.30.own_info.own), channel_id=1, source_target_pairs={{0,1},{1,2},{2,3},{3,4},{4,5},{5,6},{6,7},{7,8},{8,9},{9,10},{10,1... | collective-permute-start | bytes 405512 | tf_op jit(solution)/shard_map/ppermute | solution.py:30
  6.7 0.0 copy-start.2
  6.7 4.3 %collective-permute-start.8 = (bf16[512,128]{1,0:T(8,128)(2,1)}, bf16[512,128]{1,0:T(8,128)(2,1)S(1)}, u32[]{:S(2)}, u32[]{:S(2)}) collective-permute-start(bf16[512,128]{1,0:T(8,128)(2,1)} %get-tuple-element.41.own), channel_id=1, source_target_pairs={{0,1},{1,2},{2,3},{3,4},{4,5},{5,6},{6,7},{7,8},{8,9},{9,10},{10,1... | collective-permute-start | bytes 393224 | tf_op jit(solution)/shard_map/ppermute | solution.py:30
  11.0 0.0 copy-done.2
  11.0 1.9 %collective-permute-start.1 = (f32[1,128]{1,0:T(1,128)S(1)}, f32[1,128]{1,0:T(1,128)S(1)}, u32[]{:S(2)}, u32[]{:S(2)}) collective-permute-start(f32[1,128]{1,0:T(1,128)S(1)} %copy-done.2), channel_id=1, source_target_pairs={{0,96},{96,0},{192,288},{288,192},{384,480},{480,384},{576,672},{6... | collective-permute-start | bytes 1544 | tf_op jit(solution)/shard_map/ppermute | solution.py:34
  12.9 1.1 %collective-permute-done.1 = f32[1,128]{1,0:T(1,128)S(1)} collective-permute-done((f32[1,128]{1,0:T(1,128)S(1)}, f32[1,128]{1,0:T(1,128)S(1)}, u32[]{:S(2)}, u32[]{:S(2)}) %collective-permute-start.1) | collective-permute-done | bytes 544 | tf_op jit(solution)/shard_map/ppermute | solution.py:34
  14.0 0.0 copy-start.1
  14.0 7.4 %collective-permute-done.came1.refs_0_ = bf16[528,128]{1,0:T(8,128)(2,1)S(1)} collective-permute-done((bf16[528,128]{1,0:T(8,128)(2,1)}, bf16[528,128]{1,0:T(8,128)(2,1)S(1)}, u32[]{:S(2)}, u32[]{:S(2)}) %collective-permute-start) | collective-permute-done | bytes 135200 | tf_op jit(solution)/shard_map/ppermute | solution.py:30
  21.5 1.9 %collective-permute-start.2 = (bf16[528,128]{1,0:T(8,128)(2,1)S(1)}, bf16[528,128]{1,0:T(8,128)(2,1)S(1)}, u32[]{:S(2)}, u32[]{:S(2)}) collective-permute-start(bf16[528,128]{1,0:T(8,128)(2,1)S(1)} %collective-permute-done.came1.refs_0_), channel_id=1, source_target_pairs={{0,1},{1,2},{2,3},{3,4},{4,5},{5,6},{6,7},{7,8},{8,9},{9,10},{10,1... | collective-permute-start | bytes 405512 | tf_op jit(solution)/shard_map/ppermute | solution.py:30
  23.4 0.0 collective-permute-done.8.rest_0_
  23.4 1.9 %collective-permute-start.9 = (bf16[512,128]{1,0:T(8,128)(2,1)S(1)}, bf16[512,128]{1,0:T(8,128)(2,1)S(1)}, u32[]{:S(2)}, u32[]{:S(2)}) collective-permute-start(bf16[512,128]{1,0:T(8,128)(2,1)S(1)} %collective-permute-done.8.rest_0_), channel_id=1, source_target_pairs={{0,1},{1,2},{2,3},{3,4},{4,5},{5,6},{6,7},{7,8},{8,9},{9,10},{10,1... | collective-permute-start | bytes 393224 | tf_op jit(solution)/shard_map/ppermute | solution.py:30
  25.4 4.7 %collective-permute-start.3 = (f32[1,128]{1,0:T(1,128)S(1)}, f32[1,128]{1,0:T(1,128)S(1)}, u32[]{:S(2)}, u32[]{:S(2)}) collective-permute-start(f32[1,128]{1,0:T(1,128)S(1)} %add.15.refs_6_), channel_id=1, source_target_pairs={{192,0},{385,1},{578,2},{195,3},{388,4},{581,5},{198,6},{391,7},{5... | collective-permute-start | bytes 1544 | tf_op jit(solution)/shard_map/ppermute | solution.py:51
  30.0 1.3 %collective-permute-done.3.rest_0_.refs_7_ = f32[1,128]{1,0:T(1,128)S(1)} collective-permute-done((f32[1,128]{1,0:T(1,128)S(1)}, f32[1,128]{1,0:T(1,128)S(1)}, u32[]{:S(2)}, u32[]{:S(2)}) %collective-permute-start.3) | collective-permute-done | bytes 544 | tf_op jit(solution)/shard_map/ppermute | solution.py:51
  31.3 0.0 copy-start
  31.3 1.6 %collective-permute-done.2.came2.refs_1_ = bf16[528,128]{1,0:T(8,128)(2,1)S(1)} collective-permute-done((bf16[528,128]{1,0:T(8,128)(2,1)S(1)}, bf16[528,128]{1,0:T(8,128)(2,1)S(1)}, u32[]{:S(2)}, u32[]{:S(2)}) %collective-permute-start.2) | collective-permute-done | bytes 135200 | tf_op jit(solution)/shard_map/ppermute | solution.py:30
  32.9 2.2 %collective-permute-start.4 = (bf16[528,128]{1,0:T(8,128)(2,1)S(1)}, bf16[528,128]{1,0:T(8,128)(2,1)S(1)}, u32[]{:S(2)}, u32[]{:S(2)}) collective-permute-start(bf16[528,128]{1,0:T(8,128)(2,1)S(1)} %collective-permute-done.2.came2.refs_1_), channel_id=1, source_target_pairs={{0,1},{1,2},{2,3},{3,4},{4,5},{5,6},{6,7},{7,8},{8,9},{9,10},{10,1... | collective-permute-start | bytes 405512 | tf_op jit(solution)/shard_map/ppermute | solution.py:30
  35.1 0.0 collective-permute-done.9.rest_1_
  35.1 4.0 %collective-permute-start.10 = (bf16[512,128]{1,0:T(8,128)(2,1)S(1)}, bf16[512,128]{1,0:T(8,128)(2,1)S(1)}, u32[]{:S(2)}, u32[]{:S(2)}) collective-permute-start(bf16[512,128]{1,0:T(8,128)(2,1)S(1)} %collective-permute-done.9.rest_1_), channel_id=1, source_target_pairs={{0,1},{1,2},{2,3},{3,4},{4,5},{5,6},{6,7},{7,8},{8,9},{9,10},{10,1... | collective-permute-start | bytes 393224 | tf_op jit(solution)/shard_map/ppermute | solution.py:30
  39.1 5.0 %collective-permute-done.4.came3.refs_2_ = bf16[528,128]{1,0:T(8,128)(2,1)S(1)} collective-permute-done((bf16[528,128]{1,0:T(8,128)(2,1)S(1)}, bf16[528,128]{1,0:T(8,128)(2,1)S(1)}, u32[]{:S(2)}, u32[]{:S(2)}) %collective-permute-start.4) | collective-permute-done | bytes 135200 | tf_op jit(solution)/shard_map/ppermute | solution.py:30
  44.1 0.0 copy-done.1
  44.1 0.0 copy-done
  44.1 5.5 %attention0.1 = (bf16[128,2048]{1,0:T(8,128)(2,1)}, f32[512,128]{1,0:T(8,128)}, bf16[528,128]{1,0:T(8,128)(2,1)S(1)}, bf16[528,128]{1,0:T(8,128)(2,1)S(1)}, bf16[528,128]{1,0:T(8,128)(2,1)S(1)}) custom-call(bf16[128,4096]{1,0:T(8,128)(2,1)} %bitcast.7, bf16[128,4096]{1,0:T(8,128)(2,1)} %bitcast.9, bf16[528,128]{1,0:T(8,128)(2,1)} %get-tuple-element.30.own_info.own, ...), custom_call_target="tpu_custom_call" | custom-call | tf_op jit(solution)/shard_map/attention0/pallas_call | solution.py:336
  49.6 2.4 %collective-permute-start.5 = (bf16[528,128]{1,0:T(8,128)(2,1)S(1)}, bf16[528,128]{1,0:T(8,128)(2,1)S(1)}, u32[]{:S(2)}, u32[]{:S(2)}) collective-permute-start(bf16[528,128]{1,0:T(8,128)(2,1)S(1)} %get-tuple-element.36), channel_id=1, source_target_pairs={{0,95},{1,0},{2,1},{3,2},{4,3},{5,4},{6,5},{7,6},{8,7},{9,8},{10,9... | collective-permute-start | bytes 405512 | tf_op jit(solution)/shard_map/ppermute | solution.py:30
  51.9 0.0 collective-permute-done.10.rest_2_
  51.9 5.5 %attention1.1 = (bf16[128,2048]{1,0:T(8,128)(2,1)}, f32[512,128]{1,0:T(8,128)}, bf16[512,128]{1,0:T(8,128)(2,1)S(1)}, bf16[512,128]{1,0:T(8,128)(2,1)S(1)}, bf16[512,128]{1,0:T(8,128)(2,1)S(1)}) custom-call(bf16[128,4096]{1,0:T(8,128)(2,1)} %bitcast.8, bf16[128,4096]{1,0:T(8,128)(2,1)} %bitcast.10, bf16[528,128]{1,0:T(8,128)(2,1)} %get-tuple-element.30.own_info.own, ...), custom_call_target="tpu_custom_call" | custom-call | tf_op jit(solution)/shard_map/attention1/pallas_call | solution.py:336
  57.5 3.9 %collective-permute-start.11 = (bf16[512,128]{1,0:T(8,128)(2,1)S(1)}, bf16[512,128]{1,0:T(8,128)(2,1)S(1)}, u32[]{:S(2)}, u32[]{:S(2)}) collective-permute-start(bf16[512,128]{1,0:T(8,128)(2,1)S(1)} %get-tuple-element.46), channel_id=1, source_target_pairs={{1,0},{2,1},{3,2},{4,3},{5,4},{6,5},{7,6},{8,7},{9,8},{10,9},{11,1... | collective-permute-start | bytes 393224 | tf_op jit(solution)/shard_map/ppermute | solution.py:30
  61.4 0.0 collective-permute-done.5.refs_3_
  61.4 1.9 %collective-permute-start.6 = (bf16[528,128]{1,0:T(8,128)(2,1)S(1)}, bf16[528,128]{1,0:T(8,128)(2,1)S(1)}, u32[]{:S(2)}, u32[]{:S(2)}) collective-permute-start(bf16[528,128]{1,0:T(8,128)(2,1)S(1)} %add.16), channel_id=1, source_target_pairs={{0,95},{1,0},{2,1},{3,2},{4,3},{5,4},{6,5},{7,6},{8,7},{9,8},{10,9... | collective-permute-start | bytes 405512 | tf_op jit(solution)/shard_map/ppermute | solution.py:30
  63.4 1.4 %collective-permute-done.11 = bf16[512,128]{1,0:T(8,128)(2,1)S(1)} collective-permute-done((bf16[512,128]{1,0:T(8,128)(2,1)S(1)}, bf16[512,128]{1,0:T(8,128)(2,1)S(1)}, u32[]{:S(2)}, u32[]{:S(2)}) %collective-permute-start.11) | collective-permute-done | bytes 131104 | tf_op jit(solution)/shard_map/ppermute | solution.py:30
  64.8 6.7 %collective-permute-start.12 = (bf16[512,128]{1,0:T(8,128)(2,1)S(1)}, bf16[512,128]{1,0:T(8,128)(2,1)S(1)}, u32[]{:S(2)}, u32[]{:S(2)}) collective-permute-start(bf16[512,128]{1,0:T(8,128)(2,1)S(1)} %add.18), channel_id=1, source_target_pairs={{1,0},{2,1},{3,2},{4,3},{5,4},{6,5},{7,6},{8,7},{9,8},{10,9},{11,1... | collective-permute-start | bytes 393224 | tf_op jit(solution)/shard_map/ppermute | solution.py:30
  71.6 0.0 collective-permute-done.6.refs_4_
  71.7 2.0 %collective-permute-start.7 = (bf16[528,128]{1,0:T(8,128)(2,1)S(1)}, bf16[528,128]{1,0:T(8,128)(2,1)S(1)}, u32[]{:S(2)}, u32[]{:S(2)}) collective-permute-start(bf16[528,128]{1,0:T(8,128)(2,1)S(1)} %add.17), channel_id=1, source_target_pairs={{0,95},{1,0},{2,1},{3,2},{4,3},{5,4},{6,5},{7,6},{8,7},{9,8},{10,9... | collective-permute-start | bytes 405512 | tf_op jit(solution)/shard_map/ppermute | solution.py:30
  73.7 0.4 collective-permute-done.12
  74.1 7.7 %collective-permute-start.13 = (bf16[512,128]{1,0:T(8,128)(2,1)S(1)}, bf16[512,128]{1,0:T(8,128)(2,1)S(1)}, u32[]{:S(2)}, u32[]{:S(2)}) collective-permute-start(bf16[512,128]{1,0:T(8,128)(2,1)S(1)} %add.19), channel_id=1, source_target_pairs={{1,0},{2,1},{3,2},{4,3},{5,4},{6,5},{7,6},{8,7},{9,8},{10,9},{11,1... | collective-permute-start | bytes 393224 | tf_op jit(solution)/shard_map/ppermute | solution.py:30
  81.8 0.0 collective-permute-done.7.refs_5_
  81.8 3.0 %final.1 = (bf16[128,4096]{1,0:T(8,128)(2,1)}, bf16[128,512]{1,0:T(8,128)(2,1)}, bf16[128,512]{1,0:T(8,128)(2,1)}, f32[1,128]{1,0:T(1,128)}, f32[128,128]{1,0:T(8,128)}, /*index=5*/f32[1,48]{1,0:T(1,128)}) custom-call(bf16[528,128]{1,0:T(8,128)(2,1)} %get-tuple-element.30.own_info.own, bf16[528,128]{1,0:T(8,128)(2,1)S(1)} %collective-permute-done.came1.refs_0_, ...), custom_call_target="tpu_custom_call" | custom-call | tf_op jit(solution)/shard_map/final/pallas_call | solution.py:366
  84.8 0.0 collective-permute-done.13.came
  84.8 1.7 %rest.1 = (bf16[128,512]{1,0:T(8,128)(2,1)}, bf16[128,512]{1,0:T(8,128)(2,1)}) custom-call(f32[128,128]{1,0:T(8,128)} %get-tuple-element.44.weight, f32[512,128]{1,0:T(8,128)} %get-tuple-element.45.sum0, bf16[512,128]{1,0:T(8,128)(2,1)S(1)} %collective-permute-done.13.came, ...), custom_call_target="tpu_custom_call", output_to_operand_aliasing={{0}: (3, {}), {1}: (4, {})} | custom-call | tf_op jit(solution)/shard_map/rest/pallas_call | solution.py:394
  (5 shorter events, 0.2 us)
Async XLA Ops:
  2.4 19.1 %collective-permute-start = (bf16[528,128]{1,0:T(8,128)(2,1)}, bf16[528,128]{1,0:T(8,128)(2,1)S(1)}, u32[]{:S(2)}, u32[]{:S(2)}) collective-permute-start(bf16[528,128]{1,0:T(8,128)(2,1)} %get-tuple-element.30.own_info.own), channel_id=1, source_target_pairs={{0,1},{1,2},{2,3},{3,4},{4,5},{5,6},{6,7},{7,8},{8,9},{9,10},{10,1... | collective-permute-start | bytes 405512 | tf_op jit(solution)/shard_map/ppermute | solution.py:30
  6.7 4.3 %copy-start.2 = (f32[1,128]{1,0:T(1,128)S(1)}, f32[1,128]{1,0:T(1,128)}, u32[]{:S(2)}) copy-start(f32[1,128]{1,0:T(1,128)} %get-tuple-element.31) | copy-start | bytes 1540
  6.7 16.8 %collective-permute-start.8 = (bf16[512,128]{1,0:T(8,128)(2,1)}, bf16[512,128]{1,0:T(8,128)(2,1)S(1)}, u32[]{:S(2)}, u32[]{:S(2)}) collective-permute-start(bf16[512,128]{1,0:T(8,128)(2,1)} %get-tuple-element.41.own), channel_id=1, source_target_pairs={{0,1},{1,2},{2,3},{3,4},{4,5},{5,6},{6,7},{7,8},{8,9},{9,10},{10,1... | collective-permute-start | bytes 393224 | tf_op jit(solution)/shard_map/ppermute | solution.py:30
  11.0 3.1 %collective-permute-start.1 = (f32[1,128]{1,0:T(1,128)S(1)}, f32[1,128]{1,0:T(1,128)S(1)}, u32[]{:S(2)}, u32[]{:S(2)}) collective-permute-start(f32[1,128]{1,0:T(1,128)S(1)} %copy-done.2), channel_id=1, source_target_pairs={{0,96},{96,0},{192,288},{288,192},{384,480},{480,384},{576,672},{6... | collective-permute-start | bytes 1544 | tf_op jit(solution)/shard_map/ppermute | solution.py:34
  14.0 30.0 %copy-start.1 = (f32[1,128]{1,0:T(1,128)}, f32[1,128]{1,0:T(1,128)S(1)}, u32[]{:S(2)}) copy-start(f32[1,128]{1,0:T(1,128)S(1)} %add.15.refs_6_) | copy-start | bytes 1540
  21.5 11.4 %collective-permute-start.2 = (bf16[528,128]{1,0:T(8,128)(2,1)S(1)}, bf16[528,128]{1,0:T(8,128)(2,1)S(1)}, u32[]{:S(2)}, u32[]{:S(2)}) collective-permute-start(bf16[528,128]{1,0:T(8,128)(2,1)S(1)} %collective-permute-done.came1.refs_0_), channel_id=1, source_target_pairs={{0,1},{1,2},{2,3},{3,4},{4,5},{5,6},{6,7},{7,8},{8,9},{9,10},{10,1... | collective-permute-start | bytes 405512 | tf_op jit(solution)/shard_map/ppermute | solution.py:30
  23.4 11.6 %collective-permute-start.9 = (bf16[512,128]{1,0:T(8,128)(2,1)S(1)}, bf16[512,128]{1,0:T(8,128)(2,1)S(1)}, u32[]{:S(2)}, u32[]{:S(2)}) collective-permute-start(bf16[512,128]{1,0:T(8,128)(2,1)S(1)} %collective-permute-done.8.rest_0_), channel_id=1, source_target_pairs={{0,1},{1,2},{2,3},{3,4},{4,5},{5,6},{6,7},{7,8},{8,9},{9,10},{10,1... | collective-permute-start | bytes 393224 | tf_op jit(solution)/shard_map/ppermute | solution.py:30
  25.4 5.9 %collective-permute-start.3 = (f32[1,128]{1,0:T(1,128)S(1)}, f32[1,128]{1,0:T(1,128)S(1)}, u32[]{:S(2)}, u32[]{:S(2)}) collective-permute-start(f32[1,128]{1,0:T(1,128)S(1)} %add.15.refs_6_), channel_id=1, source_target_pairs={{192,0},{385,1},{578,2},{195,3},{388,4},{581,5},{198,6},{391,7},{5... | collective-permute-start | bytes 1544 | tf_op jit(solution)/shard_map/ppermute | solution.py:51
  31.3 12.8 %copy-start = (f32[1,128]{1,0:T(1,128)}, f32[1,128]{1,0:T(1,128)S(1)}, u32[]{:S(2)}) copy-start(f32[1,128]{1,0:T(1,128)S(1)} %collective-permute-done.3.rest_0_.refs_7_) | copy-start | bytes 1540
  32.9 11.2 %collective-permute-start.4 = (bf16[528,128]{1,0:T(8,128)(2,1)S(1)}, bf16[528,128]{1,0:T(8,128)(2,1)S(1)}, u32[]{:S(2)}, u32[]{:S(2)}) collective-permute-start(bf16[528,128]{1,0:T(8,128)(2,1)S(1)} %collective-permute-done.2.came2.refs_1_), channel_id=1, source_target_pairs={{0,1},{1,2},{2,3},{3,4},{4,5},{5,6},{6,7},{7,8},{8,9},{9,10},{10,1... | collective-permute-start | bytes 405512 | tf_op jit(solution)/shard_map/ppermute | solution.py:30
  35.1 16.9 %collective-permute-start.10 = (bf16[512,128]{1,0:T(8,128)(2,1)S(1)}, bf16[512,128]{1,0:T(8,128)(2,1)S(1)}, u32[]{:S(2)}, u32[]{:S(2)}) collective-permute-start(bf16[512,128]{1,0:T(8,128)(2,1)S(1)} %collective-permute-done.9.rest_1_), channel_id=1, source_target_pairs={{0,1},{1,2},{2,3},{3,4},{4,5},{5,6},{6,7},{7,8},{8,9},{9,10},{10,1... | collective-permute-start | bytes 393224 | tf_op jit(solution)/shard_map/ppermute | solution.py:30
  49.6 11.8 %collective-permute-start.5 = (bf16[528,128]{1,0:T(8,128)(2,1)S(1)}, bf16[528,128]{1,0:T(8,128)(2,1)S(1)}, u32[]{:S(2)}, u32[]{:S(2)}) collective-permute-start(bf16[528,128]{1,0:T(8,128)(2,1)S(1)} %get-tuple-element.36), channel_id=1, source_target_pairs={{0,95},{1,0},{2,1},{3,2},{4,3},{5,4},{6,5},{7,6},{8,7},{9,8},{10,9... | collective-permute-start | bytes 405512 | tf_op jit(solution)/shard_map/ppermute | solution.py:30
  57.5 7.3 %collective-permute-start.11 = (bf16[512,128]{1,0:T(8,128)(2,1)S(1)}, bf16[512,128]{1,0:T(8,128)(2,1)S(1)}, u32[]{:S(2)}, u32[]{:S(2)}) collective-permute-start(bf16[512,128]{1,0:T(8,128)(2,1)S(1)} %get-tuple-element.46), channel_id=1, source_target_pairs={{1,0},{2,1},{3,2},{4,3},{5,4},{6,5},{7,6},{8,7},{9,8},{10,9},{11,1... | collective-permute-start | bytes 393224 | tf_op jit(solution)/shard_map/ppermute | solution.py:30
  61.4 10.2 %collective-permute-start.6 = (bf16[528,128]{1,0:T(8,128)(2,1)S(1)}, bf16[528,128]{1,0:T(8,128)(2,1)S(1)}, u32[]{:S(2)}, u32[]{:S(2)}) collective-permute-start(bf16[528,128]{1,0:T(8,128)(2,1)S(1)} %add.16), channel_id=1, source_target_pairs={{0,95},{1,0},{2,1},{3,2},{4,3},{5,4},{6,5},{7,6},{8,7},{9,8},{10,9... | collective-permute-start | bytes 405512 | tf_op jit(solution)/shard_map/ppermute | solution.py:30
  64.8 9.3 %collective-permute-start.12 = (bf16[512,128]{1,0:T(8,128)(2,1)S(1)}, bf16[512,128]{1,0:T(8,128)(2,1)S(1)}, u32[]{:S(2)}, u32[]{:S(2)}) collective-permute-start(bf16[512,128]{1,0:T(8,128)(2,1)S(1)} %add.18), channel_id=1, source_target_pairs={{1,0},{2,1},{3,2},{4,3},{5,4},{6,5},{7,6},{8,7},{9,8},{10,9},{11,1... | collective-permute-start | bytes 393224 | tf_op jit(solution)/shard_map/ppermute | solution.py:30
  71.7 10.2 %collective-permute-start.7 = (bf16[528,128]{1,0:T(8,128)(2,1)S(1)}, bf16[528,128]{1,0:T(8,128)(2,1)S(1)}, u32[]{:S(2)}, u32[]{:S(2)}) collective-permute-start(bf16[528,128]{1,0:T(8,128)(2,1)S(1)} %add.17), channel_id=1, source_target_pairs={{0,95},{1,0},{2,1},{3,2},{4,3},{5,4},{6,5},{7,6},{8,7},{9,8},{10,9... | collective-permute-start | bytes 405512 | tf_op jit(solution)/shard_map/ppermute | solution.py:30
  74.1 10.7 %collective-permute-start.13 = (bf16[512,128]{1,0:T(8,128)(2,1)S(1)}, bf16[512,128]{1,0:T(8,128)(2,1)S(1)}, u32[]{:S(2)}, u32[]{:S(2)}) collective-permute-start(bf16[512,128]{1,0:T(8,128)(2,1)S(1)} %add.19), channel_id=1, source_target_pairs={{1,0},{2,1},{3,2},{4,3},{5,4},{6,5},{7,6},{8,7},{9,8},{10,9},{11,1... | collective-permute-start | bytes 393224 | tf_op jit(solution)/shard_map/ppermute | solution.py:30
